TPU v7x, 128 devices: a whole 4x4x4 slice. The times are simulated.
128 devices in a mesh: dp: 16 (over y_lo, x, core), blk: 8 (over y_hi, z).
Axes of the slice: x: 4, y: 4 (y_hi: 2, y_lo: 2; y = y_hi * 2 + y_lo), z: 4, core: 2. Of those that a mesh axis runs over, the one named last changes fastest.
Arguments:
- tokens: bfloat16 [1024, 3072], P('blk'), may hold values from -6 to 6
- expert_ids: int32 [1024, 2], P('blk'), may hold values from 0 to 7, all different within a row; in each aligned block of 128 rows (0 to 127, 128 to 255, ...) at most 64 rows name the same one
- gate_levels: int32 [1024, 2], P('blk'), may hold values from 1 to 255
- out_grad: bfloat16 [1024, 3072], P('blk'), may hold values from -6 to 6
- panels: bfloat16 [8, 2, 3072, 8192], P('blk', None, None, 'dp'), may hold values from -0.109375 to 0.109375
Outputs:
- token_grad: bfloat16 [1024, 3072], P('blk', 'dp')
- panel_grads: float32 [8, 2, 3072, 8192], P('blk', None, None, 'dp')
Inputs may be any that keep to these rules, and one draw needn't show every extreme that they name: `expert_ids`: the 2 experts of a token differ; among the 128 tokens of one index of blk no expert is chosen more than 64 times, and some expert is chosen exactly 64 times on some indices.
All inputs are finite; a program needn't handle non-finite values.
Results may differ from a plain program's by a relative error of at most 0.0058.
Values may be sent and summed in bfloat16 or wider, within the bound.
No kernel may reach another device: no remote copies, remote signals or barrier semaphores. Data moves between devices by JAX's collectives and lax.ppermute only.
A program may use at most 128 MiB of HBM per device.

v0:
```python
import jax
import jax.numpy as jnp
from jax import lax
from jax.sharding import PartitionSpec as P


def slot_tables(expert_ids, gate_levels, tok_count, num_experts, capacity):
    gate_frac = gate_levels.astype(jnp.float32)
    gate_frac = gate_frac / jnp.sum(gate_frac, axis=1, keepdims=True)
    flat_ids = expert_ids.reshape(-1)
    one_hot = (flat_ids[:, None] == jnp.arange(num_experts, dtype=jnp.int32)[None, :]).astype(
        jnp.int32
    )
    earlier = jnp.cumsum(one_hot, axis=0) - one_hot
    slot_pos = jnp.sum(earlier * one_hot, axis=1)
    top_count = expert_ids.shape[1]
    owner_tok = jnp.arange(flat_ids.shape[0], dtype=jnp.int32) // top_count
    slot_table = (
        jnp.full((num_experts, capacity), tok_count, jnp.int32)
        .at[flat_ids, slot_pos]
        .set(owner_tok)
    )
    slot_gate = (
        jnp.zeros((num_experts, capacity), jnp.float32)
        .at[flat_ids, slot_pos]
        .set(gate_frac.reshape(-1))
    )
    return (slot_table, slot_gate)


def dispatch(tokens, out_grad, slot_table, slot_gate):
    model_dim = tokens.shape[1]
    pad_row = jnp.zeros((1, model_dim), tokens.dtype)
    x_rows = jnp.concatenate([tokens, pad_row], axis=0)[slot_table]
    d_full = jnp.concatenate([out_grad, pad_row], axis=0)[slot_table]
    d_rows = (slot_gate[:, :, None] * d_full.astype(jnp.float32)).astype(jnp.bfloat16)
    return (x_rows, d_rows)


def gather_back(slot_table, rows, tok_count):
    width = rows.shape[-1]
    summed = (
        jnp.zeros((tok_count + 1, width), jnp.float32)
        .at[slot_table.reshape(-1)]
        .add(rows.reshape(-1, width))
    )
    return summed[:tok_count]


def shards(tokens, expert_ids, gate_levels, out_grad, panels):
    tok_count, model_dim = tokens.shape
    cycle_len = lax.axis_size("blk")
    capacity = tok_count // 2
    slot_table, slot_gate = slot_tables(expert_ids, gate_levels, tok_count, cycle_len, capacity)
    x_rows, d_rows = dispatch(tokens, out_grad, slot_table, slot_gate)
    x_recv, d_recv = (
        lax.all_to_all(x_rows, "blk", split_axis=0, concat_axis=1, tiled=True),
        lax.all_to_all(d_rows, "blk", split_axis=0, concat_axis=1, tiled=True),
    )
    x_flat = x_recv[0]
    d_flat = d_recv[0]
    w_up = panels[0, 0]
    w_down = panels[0, 1]
    pre_act = jnp.dot(x_flat, w_up, preferred_element_type=jnp.float32)
    sigma_act = jax.nn.sigmoid(pre_act)
    hidden = (pre_act * sigma_act).astype(jnp.bfloat16)
    back_h = jnp.dot(d_flat, w_down, preferred_element_type=jnp.float32)
    d_pre = (back_h * sigma_act * (1.0 + pre_act * (1.0 - sigma_act))).astype(jnp.bfloat16)
    dx_part = lax.dot_general(
        d_pre, w_up, (((1,), (1,)), ((), ())), preferred_element_type=jnp.float32
    )
    grad_up = lax.dot_general(
        x_flat, d_pre, (((0,), (0,)), ((), ())), preferred_element_type=jnp.float32
    )
    grad_down = lax.dot_general(
        d_flat, hidden, (((0,), (0,)), ((), ())), preferred_element_type=jnp.float32
    )
    panel_grads = jnp.stack([grad_up, grad_down], axis=0)[None] / jnp.float32(cycle_len)
    returned = lax.all_to_all(
        dx_part.reshape(1, cycle_len * capacity, model_dim),
        "blk",
        split_axis=1,
        concat_axis=0,
        tiled=True,
    )
    token_rows = gather_back(slot_table, returned, tok_count)
    token_grad = lax.psum_scatter(token_rows, "dp", scatter_dimension=1, tiled=True)
    return (token_grad.astype(jnp.bfloat16), panel_grads)


def solution(mesh):
    placed = (
        P("blk", None),
        P("blk", None),
        P("blk", None),
        P("blk", None),
        P("blk", None, None, "dp"),
    )
    return jax.shard_map(
        shards,
        mesh=mesh,
        in_specs=placed,
        out_specs=(P("blk", "dp"), P("blk", None, None, "dp")),
        check_vma=False,
    )
```

profile of v0, /device:TPU:0, one launch (start us, length us, event | category | flops | bytes accessed | tf_op | source)
XLA Modules:
  0.0 303.7 jit_solution(1090837421369623403)
XLA Ops:
  7.2 0.8 copy.12
  9.4 11.2 %scatter_fusion = s32[8,64]{1,0:T(8,128)S(1)} fusion(s32[8,64]{1,0:T(8,128)S(1)} %broadcast_in_dim.9, s32[256]{0:T(256)S(1)} %bitcast.47, s32[256]{0:T(256)S(1)} %and_select_fusion), kind=kCustom, calls=%fused_computation.2 | custom fusion | bytes 5120 | tf_op jit(solution)/shard_map/scatter | solution.py:21
  20.7 1.2 concatenate.19
  21.9 3.8 %gather_fusion.1 = bf16[512,3072]{1,0:T(8,128)(2,1)} fusion(bf16[129,3072]{1,0:T(8,128)(2,1)S(1)} %concatenate.19, s32[1024]{0:T(1024)S(1)} %pad_clamp_fusion), kind=kCustom, calls=%fused_computation.1 | custom fusion | bytes 6293504 | tf_op jit(solution)/shard_map/gather | solution.py:34
  25.7 8.2 %all-to-all-start.1 = ((bf16[8,64,3072]{2,1,0:T(8,128)(2,1)}), bf16[8,64,3072]{2,1,0:T(8,128)(2,1)}, u32[]{:S(2)}, u32[]{:S(2)}) async-start(bf16[8,64,3072]{2,1,0:T(8,128)(2,1)} %bitcast.49), calls=%async_computation.1 | async-start | bytes 6291456 | tf_op jit(solution)/shard_map/all_to_all | solution.py:57
  34.0 3.8 %gather_fusion = bf16[512,3072]{1,0:T(8,128)(2,1)} fusion(bf16[129,3072]{1,0:T(8,128)(2,1)S(1)} %concatenate.18, s32[1024]{0:T(1024)S(1)} %pad_clamp_fusion), kind=kCustom, calls=%fused_computation | custom fusion | bytes 6293504 | tf_op jit(solution)/shard_map/gather | solution.py:35
  38.1 11.2 %scatter_fusion.1 = f32[8,64]{1,0:T(8,128)S(1)} fusion(f32[8,64]{1,0:T(8,128)S(1)} %broadcast_in_dim.10, s32[256]{0:T(256)S(1)} %bitcast.48, f32[256]{0:T(256)S(1)} %reshape.181), kind=kCustom, calls=%fused_computation.3 | custom fusion | bytes 5120 | tf_op jit(solution)/shard_map/scatter | solution.py:26
  49.3 4.6 %fusion.3 = bf16[8,64,3072]{2,1,0:T(8,128)(2,1)} fusion(bf16[8,64,3072]{2,1,0:T(8,128)(2,1)} %bitcast.50, f32[8,64]{1,0:T(8,128)S(1)} %scatter_fusion.1), kind=kLoop, calls=%fused_computation.10 | loop fusion | flops 4718592 | bytes 6293504 | tf_op jit(solution)/shard_map/convert_element_type | solution.py:36
  53.9 17.8 %all-to-all-done.1 = bf16[8,64,3072]{2,1,0:T(8,128)(2,1)} async-done(((bf16[8,64,3072]{2,1,0:T(8,128)(2,1)}), bf16[8,64,3072]{2,1,0:T(8,128)(2,1)}, u32[]{:S(2)}, u32[]{:S(2)}) %all-to-all-start.1) | async-done | bytes 3145760 | tf_op jit(solution)/shard_map/all_to_all | solution.py:57
  71.6 4.8 %all-to-all-start = ((bf16[8,64,3072]{2,1,0:T(8,128)(2,1)}), bf16[8,64,3072]{2,1,0:T(8,128)(2,1)S(1)}, u32[]{:S(2)}, u32[]{:S(2)}) async-start(bf16[8,64,3072]{2,1,0:T(8,128)(2,1)} %fusion.3), calls=%async_computation | async-start | bytes 6291456 | tf_op jit(solution)/shard_map/all_to_all | solution.py:58
  76.4 5.6 %fusion.5 = f32[512,512]{1,0:T(8,128)} fusion(bf16[512,3072]{1,0:T(8,128)(2,1)} %bitcast.9, bf16[1,2,3072,512]{3,2,1,0:T(8,128)(2,1)} %param.9), kind=kOutput, calls=%fused_computation.15 | convolution fusion | flops 1610612736 | bytes 7340032 | tf_op jit(solution)/shard_map/dot_general | solution.py:64
  82.0 32.2 %all-to-all-done = bf16[8,64,3072]{2,1,0:T(8,128)(2,1)S(1)} async-done(((bf16[8,64,3072]{2,1,0:T(8,128)(2,1)}), bf16[8,64,3072]{2,1,0:T(8,128)(2,1)S(1)}, u32[]{:S(2)}, u32[]{:S(2)}) %all-to-all-start) | async-done | bytes 3145760 | tf_op jit(solution)/shard_map/all_to_all | solution.py:58
  114.2 5.3 %fusion.18 = bf16[512,512]{1,0:T(8,128)(2,1)S(1)} fusion(bf16[512,3072]{1,0:T(8,128)(2,1)S(1)} %bitcast.52, bf16[1,2,3072,512]{3,2,1,0:T(8,128)(2,1)} %param.9, f32[512,512]{1,0:T(8,128)} %fusion.5), kind=kOutput, calls=%fused_computation.24 | convolution fusion | flops 1612972032 | bytes 7864320 | tf_op jit(solution)/shard_map/dot_general | solution.py:67
  119.5 3.9 %convolution_bitcast_fusion.2 = f32[1,512,3072]{2,1,0:T(8,128)S(1)} fusion(bf16[512,512]{1,0:T(8,128)(2,1)S(1)} %fusion.18, bf16[1,2,3072,512]{3,2,1,0:T(8,128)(2,1)} %param.9), kind=kOutput, calls=%fused_computation.13 | convolution fusion | flops 1610612736 | bytes 9961472 | tf_op jit(solution)/shard_map/dot_general | solution.py:69
  123.5 19.0 %copy.16 = f32[1,512,3072]{2,0,1:T(1,128)} copy(f32[1,512,3072]{2,1,0:T(8,128)S(1)} %convolution_bitcast_fusion.2) | data formatting | bytes 12582912 | tf_op jit(solution)/shard_map/reshape | solution.py:80
  142.5 4.8 %all-to-all-start.2 = ((f32[1,512,3072]{2,0,1:T(1,128)}), f32[1,512,3072]{2,0,1:T(1,128)}, u32[]{:S(2)}, u32[]{:S(2)}) async-start(f32[1,512,3072]{2,0,1:T(1,128)} %copy.16), calls=%async_computation.2 | async-start | bytes 12582912 | tf_op jit(solution)/shard_map/all_to_all | solution.py:79
  147.6 71.3 %all-to-all-done.2 = f32[1,512,3072]{2,0,1:T(1,128)} async-done(((f32[1,512,3072]{2,0,1:T(1,128)}), f32[1,512,3072]{2,0,1:T(1,128)}, u32[]{:S(2)}, u32[]{:S(2)}) %all-to-all-start.2) | async-done | bytes 6291488 | tf_op jit(solution)/shard_map/all_to_all | solution.py:79
  218.9 12.8 %scatter_custom_fusion.2 = f32[129,3072]{1,0:T(8,128)S(1)} fusion(s32[512]{0:T(512)S(1)} %bitcast.56, f32[1,512,3072]{2,0,1:T(1,128)} %all-to-all-done.2, f32[]{:T(128)} %constant.14.clone.1), kind=kCustom, calls=%fused_computation.6 | custom fusion | flops 1572864 | bytes 7876612 | tf_op jit(solution)/shard_map/scatter-add | solution.py:45
  231.8 1.7 copy.18
  233.5 4.0 %convolution_bitcast_fusion.1 = f32[1,1,3072,512]{3,2,1,0:T(8,128)S(1)} fusion(bf16[512,3072]{1,0:T(8,128)(2,1)} %bitcast.9, bf16[512,512]{1,0:T(8,128)(2,1)} %copy-done.2), kind=kOutput, calls=%fused_computation.12 | convolution fusion | flops 1610612736 | bytes 9961472 | tf_op jit(solution)/shard_map/dot_general | solution.py:72
  237.6 4.6 %convolution_bitcast_fusion = f32[1,1,3072,512]{3,2,1,0:T(8,128)} fusion(bf16[512,3072]{1,0:T(8,128)(2,1)S(1)} %bitcast.53, f32[512,512]{1,0:T(8,128)S(1)} %copy-done.5), kind=kOutput, calls=%fused_computation.11 | convolution fusion | flops 1611923456 | bytes 10485760 | tf_op jit(solution)/shard_map/dot_general | solution.py:75
  242.2 9.1 %maximum_multiply_fusion = f32[1,2,3072,512]{3,2,1,0:T(8,128)} fusion(f32[1,1,3072,512]{3,2,1,0:T(8,128)} %convolution_bitcast_fusion, f32[1,1,3072,512]{3,2,1,0:T(8,128)S(1)} %convolution_bitcast_fusion.1), kind=kLoop, calls=%fused_computation.5 | loop fusion | flops 6291456 | bytes 25165824 | tf_op jit(solution)/shard_map/div | solution.py:78
  251.3 43.7 %reduce-scatter.4.cloned.1.call-done = f32[192,128]{1,0:T(8,128)} async-done(((f32[3072,128]{1,0:T(8,128)}), f32[192,128]{1,0:T(8,128)}) %reduce-scatter.4.cloned.1.call-update) | async-done | bytes 98320
  295.1 1.0 copy.19
  (39 shorter events, 3.0 us)
Async XLA Ops:
  25.7 8.2 %copy-start.3 = (bf16[128,3072]{1,0:T(8,128)(2,1)S(1)}, bf16[128,3072]{1,0:T(8,128)(2,1)}, u32[]{:S(2)}) copy-start(bf16[128,3072]{1,0:T(8,128)(2,1)} %param.8) | copy-start | bytes 2359300
  25.7 45.9 %all-to-all-start.1 = ((bf16[8,64,3072]{2,1,0:T(8,128)(2,1)}), bf16[8,64,3072]{2,1,0:T(8,128)(2,1)}, u32[]{:S(2)}, u32[]{:S(2)}) async-start(bf16[8,64,3072]{2,1,0:T(8,128)(2,1)} %bitcast.49), calls=%async_computation.1 | async-start | bytes 6291456 | tf_op jit(solution)/shard_map/all_to_all | solution.py:57
  33.9 3.8 %copy-start.4 = (s32[128,2]{0,1:T(2,128)S(1)}, s32[128,2]{0,1:T(2,128)}, u32[]{:S(2)}) copy-start(s32[128,2]{0,1:T(2,128)} %param.7) | copy-start | bytes 3076
  71.6 42.6 %all-to-all-start = ((bf16[8,64,3072]{2,1,0:T(8,128)(2,1)}), bf16[8,64,3072]{2,1,0:T(8,128)(2,1)S(1)}, u32[]{:S(2)}, u32[]{:S(2)}) async-start(bf16[8,64,3072]{2,1,0:T(8,128)(2,1)} %fusion.3), calls=%async_computation | async-start | bytes 6291456 | tf_op jit(solution)/shard_map/all_to_all | solution.py:58
  114.2 5.3 %copy-start = (bf16[8,64,3072]{2,1,0:T(8,128)(2,1)}, bf16[8,64,3072]{2,1,0:T(8,128)(2,1)S(1)}, u32[]{:S(2)}) copy-start(bf16[8,64,3072]{2,1,0:T(8,128)(2,1)S(1)} %all-to-all-done) | copy-start | bytes 9437188
  119.5 3.9 %copy-start.2 = (bf16[512,512]{1,0:T(8,128)(2,1)}, bf16[512,512]{1,0:T(8,128)(2,1)S(1)}, u32[]{:S(2)}) copy-start(bf16[512,512]{1,0:T(8,128)(2,1)S(1)} %fusion.18) | copy-start | bytes 1572868
  142.5 76.4 %all-to-all-start.2 = ((f32[1,512,3072]{2,0,1:T(1,128)}), f32[1,512,3072]{2,0,1:T(1,128)}, u32[]{:S(2)}, u32[]{:S(2)}) async-start(f32[1,512,3072]{2,0,1:T(1,128)} %copy.16), calls=%async_computation.2 | async-start | bytes 12582912 | tf_op jit(solution)/shard_map/all_to_all | solution.py:79
  147.3 147.8 %reduce-scatter.4.cloned.1.call-start = ((), (), s32[]{:S(2)}) async-start(), calls=%async_computation.4 | async-start | bytes 1671168
  233.5 4.0 %copy-start.1 = (bf16[8,64,3072]{2,1,0:T(8,128)(2,1)S(1)}, bf16[8,64,3072]{2,1,0:T(8,128)(2,1)}, u32[]{:S(2)}) copy-start(bf16[8,64,3072]{2,1,0:T(8,128)(2,1)} %copy-done) | copy-start | bytes 9437188
  233.5 4.0 %copy-start.5 = (f32[512,512]{1,0:T(8,128)S(1)}, f32[512,512]{1,0:T(8,128)}, u32[]{:S(2)}) copy-start(f32[512,512]{1,0:T(8,128)} %fusion.5) | copy-start | bytes 3145732
Sparse Core Ops, SparseCore 0:
  233.6 61.4 reduce-scatter.3
where the time goes:
time: 304 us
  waiting for transfers between devices  165 us (54%)
  local copies, waits for them, and re-layouts  55.7 us (18%)
  other arithmetic  27.3 us (9%)
  matrix products  23.5 us (8%)
  starting transfers between devices  17.9 us (6%)
  between operations  14.2 us (5%)
    all_to_all x1, waiting for transfers between devices, shards(): lax.all_to_all(dx_part.reshape(1, cycle_len * capacity, model_dim), 'blk'...  71.3 us
    unnamed x2, waiting for transfers between devices  43.8 us
    all_to_all x1, waiting for transfers between devices, shards(): lax.all_to_all(d_rows, 'blk', split_axis=0, concat_axis=1, tiled=True)  32.2 us
    reshape x1, local copies, waits for them, and re-layouts, shards(): dx_part.reshape(1, cycle_len * capacity, model_dim)  19 us
    all_to_all x1, waiting for transfers between devices, shards(): lax.all_to_all(x_rows, 'blk', split_axis=0, concat_axis=1, tiled=True)  17.8 us
    scatter-add x1, other arithmetic, gather_back(): summed = jnp.zeros((tok_count + 1, width), jnp.float32).at[slot_table.res...  12.8 us
    scatter x1, local copies, waits for them, and re-layouts, slot_tables(): slot_gate = jnp.zeros((num_experts, capacity), jnp.float32).at[flat_ids,...  11.2 us
    scatter x1, local copies, waits for them, and re-layouts, slot_tables(): slot_table = jnp.full((num_experts, capacity), tok_count, jnp.int32).at[f...  11.2 us
  transfers between devices with their start and end apart: 4, of which 4 were waited for; matrix products, arithmetic and copies ran while one was open for 14% of the time, Pallas kernels for 0%

commit v1 on v0

v1 whole, which is shorter than its diff:
```python
import jax
import jax.numpy as jnp
from jax import lax
from jax.experimental import pallas as pl
from jax.experimental.pallas import tpu as pltpu
from jax.sharding import Mesh, PartitionSpec as P

EXPERTS, CAP, TOK, D, HID = 8, 64, 128, 3072, 512
ROWS = EXPERTS * CAP
HALF = D // 2
STEP = 512
HALF_STEPS = HALF // STEP
CHIPS = 8
SLICE = D // (2 * CHIPS)
BF, F32 = jnp.bfloat16, jnp.float32
BLK = ("yhi", "z")
LIMIT = 48 * 1024 * 1024


def matmul(a, b, ca, cb):
    return lax.dot_general(a, b, (((ca,), (cb,)), ((), ())), preferred_element_type=F32)


def one_hot_rows(ids_ref, lev_ref, with_gate):
    id0, id1 = ids_ref[0:1, :], ids_ref[1:2, :]
    expert = lax.broadcasted_iota(jnp.int32, (EXPERTS, TOK), 0)
    chosen = (expert == id0) | (expert == id1)
    before = lax.broadcasted_iota(jnp.int32, (TOK, TOK), 0) < lax.broadcasted_iota(
        jnp.int32, (TOK, TOK), 1
    )
    chosen_f = jnp.where(chosen, 1.0, 0.0).astype(F32)
    before_f = jnp.where(before, 1.0, 0.0).astype(F32)
    earlier = matmul(chosen_f.astype(BF), before_f.astype(BF), 1, 0)
    slot = jnp.where(chosen, earlier, -1.0)
    place = lax.broadcasted_iota(jnp.int32, (CAP, TOK), 0).astype(F32)
    hot = jnp.concatenate(
        [jnp.where(place == slot[e : e + 1, :], 1.0, 0.0).astype(F32) for e in range(EXPERTS)],
        axis=0,
    )
    if not with_gate:
        return hot.astype(BF), None
    lev0, lev1 = lev_ref[0:1, :].astype(F32), lev_ref[1:2, :].astype(F32)
    total = lev0 + lev1
    frac = jnp.where(expert == id0, lev0 / total, jnp.where(expert == id1, lev1 / total, 0.0))
    gate = jnp.concatenate(
        [
            jnp.sum(hot[e * CAP : (e + 1) * CAP, :] * frac[e : e + 1, :], axis=1, keepdims=True)
            for e in range(EXPERTS)
        ],
        axis=0,
    )
    return hot.astype(BF), gate


def dispatch_x(core, ids, tokens):
    def body(core_ref, ids_ref, tok_ref, out_ref, hot_ref):
        @pl.when(pl.program_id(0) == 0)
        def _():
            hot_ref[...] = one_hot_rows(ids_ref, None, False)[0]

        out_ref[...] = matmul(hot_ref[...], tok_ref[...], 1, 0).astype(BF)

    return pl.pallas_call(
        body,
        grid_spec=pltpu.PrefetchScalarGridSpec(
            num_scalar_prefetch=1,
            grid=(HALF_STEPS,),
            in_specs=[
                pl.BlockSpec((2, TOK), lambda i, c: (0, 0)),
                pl.BlockSpec((TOK, STEP), lambda i, c: (0, c[0] * HALF_STEPS + i)),
            ],
            out_specs=[
                pl.BlockSpec((ROWS, STEP), lambda i, c: (0, i)),
                pl.BlockSpec((ROWS, TOK), lambda i, c: (0, 0)),
            ],
        ),
        out_shape=[
            jax.ShapeDtypeStruct((ROWS, HALF), BF),
            jax.ShapeDtypeStruct((ROWS, TOK), BF),
        ],
        compiler_params=pltpu.CompilerParams(vmem_limit_bytes=LIMIT),
    )(core, ids, tokens)


def dispatch_d(core, ids, lev, out_grad):
    def body(core_ref, ids_ref, lev_ref, grad_ref, out_ref, hot_ref, gate_ref):
        @pl.when(pl.program_id(0) == 0)
        def _():
            hot, gate = one_hot_rows(ids_ref, lev_ref, True)
            hot_ref[...] = hot
            gate_ref[...] = jnp.broadcast_to(gate, (ROWS, TOK))

        rows = matmul(hot_ref[...], grad_ref[...], 1, 0)
        out_ref[...] = (rows * gate_ref[:, 0:1]).astype(BF)

    return pl.pallas_call(
        body,
        grid_spec=pltpu.PrefetchScalarGridSpec(
            num_scalar_prefetch=1,
            grid=(HALF_STEPS,),
            in_specs=[
                pl.BlockSpec((2, TOK), lambda i, c: (0, 0)),
                pl.BlockSpec((2, TOK), lambda i, c: (0, 0)),
                pl.BlockSpec((TOK, STEP), lambda i, c: (0, c[0] * HALF_STEPS + i)),
            ],
            out_specs=pl.BlockSpec((ROWS, STEP), lambda i, c: (0, i)),
            scratch_shapes=[pltpu.VMEM((ROWS, TOK), BF), pltpu.VMEM((ROWS, TOK), F32)],
        ),
        out_shape=jax.ShapeDtypeStruct((ROWS, HALF), BF),
        compiler_params=pltpu.CompilerParams(vmem_limit_bytes=LIMIT),
    )(core, ids, lev, out_grad)


def natural(k, c):
    return jnp.where(
        k < HALF_STEPS, c * HALF_STEPS + k, (1 - c) * HALF_STEPS + k - HALF_STEPS
    )


def own_block(k):
    return jnp.minimum(k, HALF_STEPS - 1)


def oth_block(k):
    return jnp.clip(k - HALF_STEPS, 0, HALF_STEPS - 1)


def forward_up(core, x_own, x_oth, panels):
    def body(core_ref, own_ref, oth_ref, w_ref, hid_ref, slope_ref, acc_ref):
        k = pl.program_id(0)

        @pl.when(k == 0)
        def _():
            acc_ref[...] = matmul(own_ref[...], w_ref[0, 0], 1, 0)

        @pl.when((k > 0) & (k < HALF_STEPS))
        def _():
            acc_ref[...] += matmul(own_ref[...], w_ref[0, 0], 1, 0)

        @pl.when(k >= HALF_STEPS)
        def _():
            acc_ref[...] += matmul(oth_ref[...], w_ref[0, 0], 1, 0)

        @pl.when(k == 2 * HALF_STEPS - 1)
        def _():
            pre = acc_ref[...]
            sig = jax.nn.sigmoid(pre)
            hid_ref[...] = (pre * sig).astype(BF)
            slope_ref[...] = sig * (1.0 + pre * (1.0 - sig))

    return pl.pallas_call(
        body,
        grid_spec=pltpu.PrefetchScalarGridSpec(
            num_scalar_prefetch=1,
            grid=(2 * HALF_STEPS,),
            in_specs=[
                pl.BlockSpec((ROWS, STEP), lambda k, c: (0, own_block(k))),
                pl.BlockSpec((ROWS, STEP), lambda k, c: (0, oth_block(k))),
                pl.BlockSpec((1, 1, STEP, HID), lambda k, c: (0, 0, natural(k, c[0]), 0)),
            ],
            out_specs=[
                pl.BlockSpec((ROWS, HID), lambda k, c: (0, 0)),
                pl.BlockSpec((ROWS, HID), lambda k, c: (0, 0)),
            ],
            scratch_shapes=[pltpu.VMEM((ROWS, HID), F32)],
        ),
        out_shape=[
            jax.ShapeDtypeStruct((ROWS, HID), BF),
            jax.ShapeDtypeStruct((ROWS, HID), F32),
        ],
        compiler_params=pltpu.CompilerParams(vmem_limit_bytes=LIMIT),
    )(core, x_own, x_oth, panels)


DX_PARTS = 4
DX_STEPS = CHIPS // DX_PARTS


def back_down(core, d_own, d_oth, slope, panels):
    back_steps = 2 * HALF_STEPS

    def body(core_ref, own_ref, oth_ref, slope_ref, wd_ref, u0, u1, u2, u3, dpre_ref, dx_ref, acc_ref):
        k = pl.program_id(0)

        @pl.when(k == 0)
        def _():
            acc_ref[...] = matmul(own_ref[...], wd_ref[0, 0], 1, 0)

        @pl.when((k > 0) & (k < HALF_STEPS))
        def _():
            acc_ref[...] += matmul(own_ref[...], wd_ref[0, 0], 1, 0)

        @pl.when((k >= HALF_STEPS) & (k < back_steps))
        def _():
            acc_ref[...] += matmul(oth_ref[...], wd_ref[0, 0], 1, 0)

        @pl.when(k == back_steps - 1)
        def _():
            dpre_ref[...] = (acc_ref[...] * slope_ref[...]).astype(BF)

        @pl.when(k >= back_steps)
        def _():
            w = jnp.concatenate([u[0, 0] for u in (u0, u1, u2, u3)], axis=0)
            dx_ref[...] = matmul(dpre_ref[...], w, 1, 1).astype(BF)

    def up_map(q):
        def index(k, c):
            step = jnp.clip(k - back_steps, 0, DX_STEPS - 1)
            return (0, 0, (step * DX_PARTS + q) * 2 + 1 - c[0], 0)

        return index

    def bk(k):
        return jnp.minimum(k, back_steps - 1)

    return pl.pallas_call(
        body,
        grid_spec=pltpu.PrefetchScalarGridSpec(
            num_scalar_prefetch=1,
            grid=(back_steps + DX_STEPS,),
            in_specs=[
                pl.BlockSpec((ROWS, STEP), lambda k, c: (0, own_block(k))),
                pl.BlockSpec((ROWS, STEP), lambda k, c: (0, oth_block(k))),
                pl.BlockSpec((ROWS, HID), lambda k, c: (0, 0)),
                pl.BlockSpec((1, 1, STEP, HID), lambda k, c: (0, 1, natural(bk(k), c[0]), 0)),
            ]
            + [pl.BlockSpec((1, 1, SLICE, HID), up_map(q)) for q in range(DX_PARTS)],
            out_specs=[
                pl.BlockSpec((ROWS, HID), lambda k, c: (0, 0)),
                pl.BlockSpec(
                    (ROWS, DX_PARTS * SLICE),
                    lambda k, c: (0, jnp.clip(k - back_steps, 0, DX_STEPS - 1)),
                ),
            ],
            scratch_shapes=[pltpu.VMEM((ROWS, HID), F32)],
        ),
        out_shape=[
            jax.ShapeDtypeStruct((ROWS, HID), BF),
            jax.ShapeDtypeStruct((ROWS, HALF), BF),
        ],
        compiler_params=pltpu.CompilerParams(vmem_limit_bytes=LIMIT),
    )(core, d_own, d_oth, slope, panels, panels, panels, panels, panels)


def dx_mine(core, d_pre, panels):
    def body(core_ref, dpre_ref, u0, u1, u2, u3, dx_ref):
        w = jnp.concatenate([u[0, 0] for u in (u0, u1, u2, u3)], axis=0)
        dx_ref[...] = matmul(dpre_ref[...], w, 1, 1)

    def up_map(q):
        return lambda k, c: (0, 0, (k * DX_PARTS + q) * 2 + c[0], 0)

    return pl.pallas_call(
        body,
        grid_spec=pltpu.PrefetchScalarGridSpec(
            num_scalar_prefetch=1,
            grid=(DX_STEPS,),
            in_specs=[pl.BlockSpec((ROWS, HID), lambda k, c: (0, 0))]
            + [pl.BlockSpec((1, 1, SLICE, HID), up_map(q)) for q in range(DX_PARTS)],
            out_specs=pl.BlockSpec((ROWS, DX_PARTS * SLICE), lambda k, c: (0, k)),
        ),
        out_shape=jax.ShapeDtypeStruct((ROWS, HALF), F32),
        compiler_params=pltpu.CompilerParams(vmem_limit_bytes=LIMIT),
    )(core, d_pre, panels, panels, panels, panels)


def weight_grads(core, x_own, x_oth, d_own, d_oth, d_pre, hidden):
    def body(core_ref, xo, xt, do, dt, dpre_ref, hid_ref, out_ref):
        g, k = pl.program_id(0), pl.program_id(1)
        cases = (
            (0, True, xo, dpre_ref),
            (0, False, xt, dpre_ref),
            (1, True, do, hid_ref),
            (1, False, dt, hid_ref),
        )
        for which, own, lhs, rhs in cases:

            @pl.when((g == which) & ((k < HALF_STEPS) == own))
            def _(lhs=lhs, rhs=rhs):
                out_ref[0, 0] = matmul(lhs[...], rhs[...], 0, 0) * (1.0 / EXPERTS)

    last = HALF_STEPS - 1

    def at(own, which):
        def index(g, k, c):
            block = own_block(k) if own else oth_block(k)
            return (0, jnp.where(g == which, block, last if which == 0 else 0))

        return pl.BlockSpec((ROWS, STEP), index)

    whole = pl.BlockSpec((ROWS, HID), lambda g, k, c: (0, 0))
    return pl.pallas_call(
        body,
        grid_spec=pltpu.PrefetchScalarGridSpec(
            num_scalar_prefetch=1,
            grid=(2, 2 * HALF_STEPS),
            in_specs=[at(True, 0), at(False, 0), at(True, 1), at(False, 1), whole, whole],
            out_specs=pl.BlockSpec(
                (1, 1, STEP, HID), lambda g, k, c: (0, g, natural(k, c[0]), 0)
            ),
        ),
        out_shape=jax.ShapeDtypeStruct((1, 2, D, HID), F32),
        compiler_params=pltpu.CompilerParams(vmem_limit_bytes=LIMIT),
        cost_estimate=pl.CostEstimate(
            flops=4 * ROWS * D * HID, transcendentals=0, bytes_accessed=8 * D * HID + 4 * ROWS * D
        ),
    )(core, x_own, x_oth, d_own, d_oth, d_pre, hidden)


def shards(tokens, expert_ids, gate_levels, out_grad, panels):
    core = lax.axis_index("core").astype(jnp.int32).reshape(1)
    ids, lev = expert_ids.T, gate_levels.T
    swap = [(0, 1), (1, 0)]

    def to_experts(rows):
        rows = rows.reshape(EXPERTS, CAP, HALF)
        own = lax.all_to_all(rows, BLK, split_axis=0, concat_axis=0, tiled=True)
        own = own.reshape(ROWS, HALF)
        return own, lax.ppermute(own, "core", swap)

    x_rows, hot = dispatch_x(core, ids, tokens)
    d_rows = dispatch_d(core, ids, lev, out_grad)
    x_own, x_oth = to_experts(x_rows)
    d_own, d_oth = to_experts(d_rows)
    hidden, slope = forward_up(core, x_own, x_oth, panels)
    d_pre, dx_send = back_down(core, d_own, d_oth, slope, panels)
    dx_recv = lax.ppermute(dx_send, "core", swap)
    dx_own = dx_mine(core, d_pre, panels)
    chip_dx = (dx_own + dx_recv.astype(F32)).astype(BF).reshape(EXPERTS, CAP, HALF)
    back = lax.all_to_all(chip_dx, BLK, split_axis=0, concat_axis=0, tiled=True)
    panel_grads = weight_grads(core, x_own, x_oth, d_own, d_oth, d_pre, hidden)
    tok_t = matmul(back.reshape(ROWS, HALF), hot, 0, 0).astype(BF)
    parts = lax.all_to_all(
        tok_t.reshape(CHIPS, SLICE, TOK), ("ylo", "x"), split_axis=0, concat_axis=0, tiled=True
    )
    token_grad = jnp.sum(parts.astype(F32), axis=0).T.astype(BF)
    return token_grad, panel_grads


def solution(mesh):
    fine = Mesh(mesh.devices.reshape(2, 4, 2, 2, 4), ("ylo", "x", "core", "yhi", "z"))
    dp = ("ylo", "x", "core")
    rows = P(BLK, None)
    return jax.shard_map(
        shards,
        mesh=fine,
        in_specs=(rows, rows, rows, rows, P(BLK, None, None, dp)),
        out_specs=(P(BLK, dp), P(BLK, None, None, dp)),
        check_vma=False,
    )
```

time: 304 us -> 129 us (0.42)
  waiting for transfers between devices: 165 us -> 38.4 us
  local copies, waits for them, and re-layouts: 55.7 us -> 9.24 us
  Pallas kernels: 0 us -> 31 us
  blocking collectives: 0 us -> 27.8 us
  other arithmetic: 27.3 us -> 1.24 us
  matrix products: 23.5 us -> 1.36 us
  between operations: 14.2 us -> 0.77 us
    all_to_all x3, waiting for transfers between devices: 121 us -> 38 us  [the longest x2 38 us: to_experts(): own = lax.all_to_all(rows, BLK, split_axis=0, concat_axis=0, tiled=True)]
    unnamed x2 -> x0, waiting for transfers between devices: 43.8 us -> none
    pallas_call x0 -> x6, Pallas kernels: none -> 31 us  [the longest x1 11.6 us: weight_grads(): pl.pallas_call(body, grid_spec=pltpu.PrefetchScalarGridSpec(num_scalar_pr...]
    all_to_all x0 -> x1, blocking collectives: none -> 27.8 us  [shards(): back = lax.all_to_all(chip_dx, BLK, split_axis=0, concat_axis=0, tiled=True)]
    scatter x2 -> x0, local copies, waits for them, and re-layouts: 22.4 us -> none  [the longest x1 11.2 us: slot_tables(): slot_gate = jnp.zeros((num_experts, capacity), jnp.float32).at[flat_ids,...]
    dot_general x5 -> x1, matrix products: 23.5 us -> 1.36 us  [matmul(): lax.dot_general(a, b, (((ca,), (cb,)), ((), ())), preferred_element_type=...]
    reshape x4 -> x0, local copies, waits for them, and re-layouts: 19.4 us -> none  [the longest x1 19 us: shards(): dx_part.reshape(1, cycle_len * capacity, model_dim)]
    scatter-add x1 -> x0, other arithmetic: 12.8 us -> none  [gather_back(): summed = jnp.zeros((tok_count + 1, width), jnp.float32).at[slot_table.res...]
  transfers between devices with their start and end apart: 4 -> 6, of which waited for: 4 -> 3; matrix products, arithmetic and copies ran while one was open for 14% -> 0% of each run, Pallas kernels for 0% -> 17%
where the time goes in v1:
time: 129 us; the launch traced here: 128 us
  waiting for transfers between devices  38.4 us (30%)
  Pallas kernels  31 us (24%)
  blocking collectives  27.8 us (22%)
  starting transfers between devices  17.9 us (14%)
  local copies, waits for them, and re-layouts  9.24 us (7%)
  matrix products  1.36 us (1%)
    all_to_all x2, waiting for transfers between devices, to_experts(): own = lax.all_to_all(rows, BLK, split_axis=0, concat_axis=0, tiled=True)  38 us
    all_to_all x1, blocking collectives, shards(): back = lax.all_to_all(chip_dx, BLK, split_axis=0, concat_axis=0, tiled=True)  27.8 us
    all_to_all x2, starting transfers between devices, to_experts(): own = lax.all_to_all(rows, BLK, split_axis=0, concat_axis=0, tiled=True)  12.9 us
    pallas_call x1, Pallas kernels, weight_grads(): pl.pallas_call(body, grid_spec=pltpu.PrefetchScalarGridSpec(num_scalar_pr...  11.6 us
    unnamed x24, local copies, waits for them, and re-layouts  9.24 us
    pallas_call x1, Pallas kernels, back_down(): pl.pallas_call(body, grid_spec=pltpu.PrefetchScalarGridSpec(num_scalar_pr...  8.18 us
    pallas_call x1, Pallas kernels, forward_up(): pl.pallas_call(body, grid_spec=pltpu.PrefetchScalarGridSpec(num_scalar_pr...  5.94 us
    all_to_all x1, starting transfers between devices, shards(): lax.all_to_all(tok_t.reshape(CHIPS, SLICE, TOK), ('ylo', 'x'), split_axis...  4.41 us
  transfers between devices with their start and end apart: 6, of which 3 were waited for; matrix products, arithmetic and copies ran while one was open for 0% of the time, Pallas kernels for 17%

profile of v1, /device:TPU:0, one launch (start us, length us, event | category | flops | bytes accessed | tf_op | source)
XLA Modules:
  0.0 127.6 jit_solution(2401311499768247588)
XLA Ops:
  0.6 1.1 copy-done.4
  1.8 0.7 copy-done.8
  2.4 1.2 shard_map.69
  3.6 1.2 copy-done.3
  4.8 8.2 %all-to-all-start.1 = ((bf16[8,64,1536]{2,1,0:T(8,128)(2,1)}), bf16[8,64,1536]{2,1,0:T(8,128)(2,1)S(1)}, u32[]{:S(2)}, u32[]{:S(2)}) async-start(bf16[8,64,1536]{2,1,0:T(8,128)(2,1)} %bitcast.20), calls=%async_computation.1 | async-start | bytes 3145728 | tf_op jit(solution)/shard_map/all_to_all | solution.py:317
  13.0 1.1 copy-done.5
  14.1 1.4 %shard_map.68 = bf16[512,1536]{1,0:T(8,128)(2,1)S(1)} custom-call(s32[1]{0:T(128)} %bitcast.core_ref, s32[2,128]{1,0:T(2,128)S(1)} %bitcast.22, s32[2,128]{1,0:T(2,128)S(1)} %bitcast.23, bf16[128,3072]{1,0:T(8,128)(2,1)S(1)} %copy-done.5), custom_call_target="tpu_custom_call" | custom-call | tf_op jit(solution)/shard_map/pallas_call | solution.py:96
  15.6 1.1 copy-done
  16.7 17.1 %all-to-all-done.1 = bf16[8,64,1536]{2,1,0:T(8,128)(2,1)S(1)} async-done(((bf16[8,64,1536]{2,1,0:T(8,128)(2,1)}), bf16[8,64,1536]{2,1,0:T(8,128)(2,1)S(1)}, u32[]{:S(2)}, u32[]{:S(2)}) %all-to-all-start.1) | async-done | bytes 1572896 | tf_op jit(solution)/shard_map/all_to_all | solution.py:317
  33.8 4.8 %all-to-all-start = ((bf16[8,64,1536]{2,1,0:T(8,128)(2,1)}), bf16[8,64,1536]{2,1,0:T(8,128)(2,1)S(1)}, u32[]{:S(2)}, u32[]{:S(2)}) async-start(bf16[8,64,1536]{2,1,0:T(8,128)(2,1)} %bitcast.19), calls=%async_computation | async-start | bytes 3145728 | tf_op jit(solution)/shard_map/all_to_all | solution.py:317
  38.5 21.0 %all-to-all-done = bf16[8,64,1536]{2,1,0:T(8,128)(2,1)S(1)} async-done(((bf16[8,64,1536]{2,1,0:T(8,128)(2,1)}), bf16[8,64,1536]{2,1,0:T(8,128)(2,1)S(1)}, u32[]{:S(2)}, u32[]{:S(2)}) %all-to-all-start) | async-done | bytes 1572896 | tf_op jit(solution)/shard_map/all_to_all | solution.py:317
  59.5 5.9 %shard_map.70 = (bf16[512,512]{1,0:T(8,128)(2,1)S(1)}, f32[512,512]{1,0:T(8,128)S(1)}) custom-call(s32[1]{0:T(128)} %bitcast.core_ref, bf16[512,1536]{1,0:T(8,128)(2,1)S(1)} %bitcast.17, bf16[512,1536]{1,0:T(8,128)(2,1)} %collective-permute-done.1.oth_ref.xt, bf16[1,2,3072,512]{3,2,1,0:T(8,128)(2,1)} %u3.3), custom_call_target="tpu_custom_call" | custom-call | tf_op jit(solution)/shard_map/pallas_call | solution.py:151
  65.5 0.8 copy-done.6
  66.2 1.1 copy-done.11
  67.4 8.2 %shard_map.71 = (bf16[512,512]{1,0:T(8,128)(2,1)S(1)}, bf16[512,1536]{1,0:T(8,128)(2,1)S(1)}) custom-call(s32[1]{0:T(128)} %bitcast.core_ref, bf16[512,1536]{1,0:T(8,128)(2,1)S(1)} %bitcast.14, bf16[512,1536]{1,0:T(8,128)(2,1)} %copy-done.11, f32[512,512]{1,0:T(8,128)S(1)} %get-tuple-element.9.slope_ref, bf16[1,2,3072,512]{3,2,1,0:T(8,128)(2,1)} %u3.3, ...), custom_call_target="tpu_custom_call" | custom-call | tf_op jit(solution)/shard_map/pallas_call | solution.py:216
  76.1 2.7 %shard_map.72 = f32[512,1536]{1,0:T(8,128)S(1)} custom-call(s32[1]{0:T(128)} %bitcast.core_ref, bf16[512,512]{1,0:T(8,128)(2,1)S(1)} %get-tuple-element.10.dpre_ref, bf16[1,2,3072,512]{3,2,1,0:T(8,128)(2,1)} %u3.3, bf16[1,2,3072,512]{3,2,1,0:T(8,128)(2,1)} %u3.3, bf16[1,2,3072,512]{3,2,1,0:T(8,128)(2,1)} %u3.3, bf16[1,2,3072,512]{3,2,1,0:T(8,128)(2,1)} %u3.3), custom_call_target="tpu_custom_call" | custom-call | tf_op jit(solution)/shard_map/pallas_call | solution.py:253
  79.2 0.6 add_convert_fusion
  79.7 27.8 %all_to_all.20 = bf16[8,64,1536]{2,1,0:T(8,128)(2,1)S(1)} all-to-all(bf16[8,64,1536]{2,1,0:T(8,128)(2,1)S(1)} %bitcast.25), channel_id=1, replica_groups=mesh['ylo'=2,'x'=4,'core'=2,'yhi'=2,'z'=4] {'yhi','z'}, dimensions={0} | all-to-all | bytes 3145728 | tf_op jit(solution)/shard_map/all_to_all | solution.py:330
  107.5 1.4 %convolution_convert_fusion = bf16[1536,128]{1,0:T(8,128)(2,1)} fusion(bf16[512,1536]{1,0:T(8,128)(2,1)S(1)} %bitcast.24, bf16[512,128]{1,0:T(8,128)(2,1)S(1)} %get-tuple-element.12), kind=kOutput, calls=%fused_computation.1 | convolution fusion | flops 201523200 | bytes 2097152 | tf_op jit(solution)/shard_map/dot_general | solution.py:21
  108.9 4.4 %all-to-all-start.3 = ((bf16[8,192,128]{2,1,0:T(8,128)(2,1)}), bf16[8,192,128]{2,1,0:T(8,128)(2,1)S(1)}, u32[]{:S(2)}, u32[]{:S(2)}) async-start(bf16[8,192,128]{2,1,0:T(8,128)(2,1)} %bitcast.26), calls=%async_computation.3 | async-start | bytes 786432 | tf_op jit(solution)/shard_map/all_to_all | solution.py:333
  113.3 1.0 copy-done.2
  114.4 1.0 copy-done.7
  115.4 11.6 %shard_map.73 = f32[1,2,3072,512]{3,2,1,0:T(8,128)} custom-call(s32[1]{0:T(128)} %bitcast.core_ref, bf16[512,1536]{1,0:T(8,128)(2,1)S(1)} %bitcast.18, bf16[512,1536]{1,0:T(8,128)(2,1)} %collective-permute-done.1.oth_ref.xt, bf16[512,1536]{1,0:T(8,128)(2,1)S(1)} %bitcast.15, bf16[512,1536]{1,0:T(8,128)(2,1)} %copy-done.11, bf16[512,512]{1,0:T(8,128)(2,1)S(1)} %copy-done.2, ...), custom_call_target="tpu_custom_call" | custom-call | flops 3221225472 | bytes 18874368 | tf_op jit(solution)/shard_map/pallas_call | solution.py:292
  127.0 0.7 reduce_sum.12
  (22 shorter events, 0.9 us)
Async XLA Ops:
  0.6 1.1 copy-start.4
  1.8 0.7 copy-start.8
  3.6 1.2 copy-start.3
  4.8 8.2 %copy-start.9 = (s32[128,2]{0,1:T(2,128)S(1)}, s32[128,2]{0,1:T(2,128)}, u32[]{:S(2)}) copy-start(s32[128,2]{0,1:T(2,128)} %param.6) | copy-start | bytes 3076
  4.8 8.2 %copy-start.10 = (s32[128,2]{0,1:T(2,128)S(1)}, s32[128,2]{0,1:T(2,128)}, u32[]{:S(2)}) copy-start(s32[128,2]{0,1:T(2,128)} %param.7) | copy-start | bytes 3076
  4.8 29.0 %all-to-all-start.1 = ((bf16[8,64,1536]{2,1,0:T(8,128)(2,1)}), bf16[8,64,1536]{2,1,0:T(8,128)(2,1)S(1)}, u32[]{:S(2)}, u32[]{:S(2)}) async-start(bf16[8,64,1536]{2,1,0:T(8,128)(2,1)} %bitcast.20), calls=%async_computation.1 | async-start | bytes 3145728 | tf_op jit(solution)/shard_map/all_to_all | solution.py:317
  13.0 1.1 copy-start.5
  15.6 1.1 copy-start
  33.8 25.7 %all-to-all-start = ((bf16[8,64,1536]{2,1,0:T(8,128)(2,1)}), bf16[8,64,1536]{2,1,0:T(8,128)(2,1)S(1)}, u32[]{:S(2)}, u32[]{:S(2)}) async-start(bf16[8,64,1536]{2,1,0:T(8,128)(2,1)} %bitcast.19), calls=%async_computation | async-start | bytes 3145728 | tf_op jit(solution)/shard_map/all_to_all | solution.py:317
  38.5 21.0 %collective-permute-start.1 = (bf16[512,1536]{1,0:T(8,128)(2,1)S(1)}, bf16[512,1536]{1,0:T(8,128)(2,1)}, u32[]{:S(2)}, u32[]{:S(2)}) collective-permute-start(bf16[512,1536]{1,0:T(8,128)(2,1)S(1)} %bitcast.16), channel_id=1, source_target_pairs={{0,8},{8,0},{1,9},{9,1},{2,10},{10,2},{3,11},{11,3},{4,12},{12,4},... | collective-permute-start | bytes 4718600 | tf_op jit(solution)/shard_map/ppermute | solution.py:319
  59.5 6.7 %collective-permute-start = (bf16[512,1536]{1,0:T(8,128)(2,1)S(1)}, bf16[512,1536]{1,0:T(8,128)(2,1)S(1)}, u32[]{:S(2)}, u32[]{:S(2)}) collective-permute-start(bf16[512,1536]{1,0:T(8,128)(2,1)S(1)} %bitcast.13), channel_id=1, source_target_pairs={{0,8},{8,0},{1,9},{9,1},{2,10},{10,2},{3,11},{11,3},{4,12},{12,4},... | collective-permute-start | bytes 4718600 | tf_op jit(solution)/shard_map/ppermute | solution.py:319
  65.5 0.8 copy-start.6
  66.2 1.1 copy-start.11
  75.6 3.3 %copy-start.1 = (bf16[512,512]{1,0:T(8,128)(2,1)}, bf16[512,512]{1,0:T(8,128)(2,1)S(1)}, u32[]{:S(2)}) copy-start(bf16[512,512]{1,0:T(8,128)(2,1)S(1)} %get-tuple-element.10.dpre_ref) | copy-start | bytes 1572868
  75.6 3.6 %collective-permute-start.2 = (bf16[512,1536]{1,0:T(8,128)(2,1)S(1)}, bf16[512,1536]{1,0:T(8,128)(2,1)S(1)}, u32[]{:S(2)}, u32[]{:S(2)}) collective-permute-start(bf16[512,1536]{1,0:T(8,128)(2,1)S(1)} %get-tuple-element.11), channel_id=1, source_target_pairs={{0,8},{8,0},{1,9},{9,1},{2,10},{10,2},{3,11},{11,3},{4,12},{12,4},... | collective-permute-start | bytes 4718600 | tf_op jit(solution)/shard_map/ppermute | solution.py:327
  108.9 18.1 %all-to-all-start.3 = ((bf16[8,192,128]{2,1,0:T(8,128)(2,1)}), bf16[8,192,128]{2,1,0:T(8,128)(2,1)S(1)}, u32[]{:S(2)}, u32[]{:S(2)}) async-start(bf16[8,192,128]{2,1,0:T(8,128)(2,1)} %bitcast.26), calls=%async_computation.3 | async-start | bytes 786432 | tf_op jit(solution)/shard_map/all_to_all | solution.py:333
  113.3 1.0 copy-start.2
  114.4 1.0 copy-start.7

commit v2 on v0

v2 whole, which is shorter than its diff:
```python
import jax
import jax.numpy as jnp
from jax import lax
from jax.experimental import pallas as pl
from jax.experimental.pallas import tpu as pltpu
from jax.sharding import Mesh, PartitionSpec as P

EXPERTS, CAP, TOK, D, HID = 8, 64, 128, 3072, 512
ROWS = EXPERTS * CAP
HALF = D // 2
XS = 4
QUART = HALF // XS
CHIPS = 8
SLICE = D // (2 * CHIPS)
LANES = 128
REST = SLICE - LANES
PACK = CAP * SLICE // LANES
DESTS = EXPERTS * CHIPS
BF, F32 = jnp.bfloat16, jnp.float32
BLK = ("yhi", "z")
AXES = ("ylo", "x", "core", "yhi", "z")
SIZES = (2, 4, 2, 2, 4)
MIB = 1024 * 1024


def matmul(a, b, ca, cb):
    return lax.dot_general(a, b, (((ca,), (cb,)), ((), ())), preferred_element_type=F32)


VM = pl.BlockSpec(memory_space=pltpu.VMEM)
SM = pl.BlockSpec(memory_space=pltpu.SMEM)
HB = pl.BlockSpec(memory_space=pltpu.HBM)
ANY = pl.BlockSpec(memory_space=pl.ANY)
DMA = pltpu.SemaphoreType.DMA


def call(body, ins, outs, scratch, limit=20, flops=0, nbytes=0, **kw):
    return pl.pallas_call(
        body,
        in_specs=ins,
        out_specs=[VM] * len(outs),
        out_shape=[jax.ShapeDtypeStruct(s, t) for s, t in outs],
        scratch_shapes=scratch,
        compiler_params=pltpu.CompilerParams(vmem_limit_bytes=limit * MIB),
        cost_estimate=pl.CostEstimate(flops=flops, transcendentals=0, bytes_accessed=nbytes),
        **kw,
    )


def slot_rows(table):
    expert = lax.broadcasted_iota(jnp.int32, (EXPERTS, TOK), 0)
    chosen = (expert == table[0:1, :]) | (expert == table[1:2, :])
    before = lax.broadcasted_iota(jnp.int32, (TOK, TOK), 0) < lax.broadcasted_iota(
        jnp.int32, (TOK, TOK), 1
    )
    earlier = matmul(
        jnp.where(chosen, 1.0, 0.0).astype(BF), jnp.where(before, 1.0, 0.0).astype(BF), 1, 0
    )
    return expert, jnp.where(chosen, earlier, -1.0)


def hot_chunk(slot, e):
    place = lax.broadcasted_iota(jnp.int32, (CAP, TOK), 0).astype(F32)
    return jnp.where(place == slot[e : e + 1, :], 1.0, 0.0).astype(F32)


def dispatch_x(table, tokens):
    def body(table_ref, tok_ref, out_ref, hot_ref):
        _, slot = slot_rows(table_ref[...])
        for e in range(EXPERTS):
            hot_ref[e * CAP : (e + 1) * CAP, :] = hot_chunk(slot, e).astype(BF)
        out_ref[...] = matmul(hot_ref[...], tok_ref[...], 1, 0).astype(BF)

    return call(body, [VM, VM], [((ROWS, HALF), BF), ((ROWS, TOK), BF)], [])(table, tokens)


def dispatch_d(table, out_grad):
    def body(table_ref, grad_ref, out_ref, hot_ref, gate_ref):
        table = table_ref[...]
        expert, slot = slot_rows(table)
        lev = table[2:4, :].astype(F32)
        frac = lev / (lev[0:1, :] + lev[1:2, :])
        frac = jnp.where(
            expert == table[0:1, :],
            frac[0:1, :],
            jnp.where(expert == table[1:2, :], frac[1:2, :], 0.0),
        )
        for e in range(EXPERTS):
            rows = slice(e * CAP, (e + 1) * CAP)
            hot = hot_chunk(slot, e)
            hot_ref[rows, :] = hot.astype(BF)
            gate = jnp.sum(hot * frac[e : e + 1, :], axis=1, keepdims=True)
            gate_ref[rows, :] = jnp.broadcast_to(gate, (CAP, LANES))
        rows = matmul(hot_ref[...], grad_ref[...], 1, 0)
        out_ref[...] = (rows * gate_ref[:, 0:1]).astype(BF)

    return call(
        body,
        [VM, VM],
        [((ROWS, QUART), BF)],
        [pltpu.VMEM((ROWS, TOK), BF), pltpu.VMEM((ROWS, LANES), F32)],
    )(table, out_grad)[0]


def assemble(pieces):
    def body(*refs):
        for r in range(XS):
            refs[XS][:, r * QUART : (r + 1) * QUART] = refs[r][...]

    return call(body, [VM] * XS, [((ROWS, HALF), BF)], [])(*pieces)[0]


TIGHT = 59


def panel_rows(panel_ref, which, start, unit, count, buf, into, sem):
    rows = pl.ds(pl.multiple_of(start, unit), count)
    copy = pltpu.make_async_copy(panel_ref.at[0, which, rows, :], buf.at[pl.ds(into, count), :], sem)
    copy.start()
    return copy


def owned_rows(panel_ref, o, buf, sems):
    copies = []
    for j in range(CHIPS):
        first = (2 * j + o) * SLICE
        copies.append(panel_rows(panel_ref, 0, first, 64, LANES, buf, j * LANES, sems.at[2 * j]))
        copies.append(
            panel_rows(
                panel_ref, 0, first + LANES, 64, REST, buf, CHIPS * LANES + j * REST, sems.at[2 * j + 1]
            )
        )
    return copies


PARTS = 3
PART = HALF // PARTS


def half_rows(panel_ref, o, buf, sems):
    return [
        panel_rows(panel_ref, 0, o * HALF + i * PART, PART, PART, buf, i * PART, sems.at[i])
        for i in range(PARTS)
    ]


def back_full(place, d_own, d_oth, panels):
    def body(place_ref, own_ref, oth_ref, panel_ref, out_ref, buf, sems):
        copies = []
        for side in range(2):
            o = (place_ref[0] + side) % 2
            for r in range(XS):
                start = (o * XS + (place_ref[1] + XS - r) % XS) * QUART
                i = side * XS + r
                copies.append(
                    panel_rows(panel_ref, 1, start, QUART, QUART, buf, i * QUART, sems.at[i])
                )
        for c in copies[:XS]:
            c.wait()
        own = matmul(own_ref[...], buf[:HALF, :], 1, 0)
        for c in copies[XS:]:
            c.wait()
        out_ref[...] = own + matmul(oth_ref[...], buf[HALF:, :], 1, 0)

    return call(
        body,
        [SM, VM, VM, HB],
        [((ROWS, HID), F32)],
        [pltpu.VMEM((D, HID), BF), DMA((2 * XS,))],
        limit=TIGHT,
        flops=2 * ROWS * D * HID,
        nbytes=2 * D * HID,
    )(place, d_own, d_oth, panels)[0]


def up_own(place, x_own, panels):
    def body(place_ref, own_ref, panel_ref, out_ref, buf, sems):
        for c in half_rows(panel_ref, place_ref[0], buf, sems):
            c.wait()
        out_ref[...] = matmul(own_ref[...], buf[...], 1, 0)

    return call(
        body,
        [SM, VM, HB],
        [((ROWS, HID), F32)],
        [pltpu.VMEM((HALF, HID), BF), DMA((PARTS,))],
        limit=TIGHT,
        flops=ROWS * D * HID,
        nbytes=D * HID,
    )(place, x_own, panels)[0]


def packed_dx(dpre_ref, owned_ref, out_ref):
    out_t = out_ref.dtype
    first = CHIPS * LANES
    wide = matmul(dpre_ref[...], owned_ref[:first, :], 1, 1)
    narrow = matmul(dpre_ref[...], owned_ref[first:, :], 1, 1)
    left = lax.broadcasted_iota(jnp.int32, (EXPERTS, CAP // 2, LANES), 2) < REST
    for j in range(CHIPS):
        part = wide[:, j * LANES : (j + 1) * LANES].astype(out_t)
        out_ref[:, j, 0:CAP, :] = part.reshape(EXPERTS, CAP, LANES)
    for m in range(CHIPS // 2):
        here = narrow[:, m * LANES : (m + 1) * LANES]
        there = pltpu.roll(here, REST, 1)
        here = here.reshape(EXPERTS, CAP, LANES)
        there = there.reshape(EXPERTS, CAP, LANES)
        lo, hi = slice(0, CAP // 2), slice(CAP // 2, CAP)
        even = jnp.where(left, here[:, lo, :], there[:, hi, :])
        odd = jnp.where(left, there[:, lo, :], here[:, hi, :])
        out_ref[:, 2 * m, CAP:PACK, :] = even.astype(out_t)
        out_ref[:, 2 * m + 1, CAP:PACK, :] = odd.astype(out_t)


def middle(place, part, x_oth, back, panels):
    def body(place_ref, part_ref, oth_ref, back_ref, panel_ref, hid_ref, dpre_ref, dx_ref, *tmp):
        up, owned, up_sems, sems = tmp
        other = 1 - place_ref[0]
        ups = half_rows(panel_ref, other, up, up_sems)
        copies = owned_rows(panel_ref, other, owned, sems)
        for c in ups:
            c.wait()
        pre = part_ref[...] + matmul(oth_ref[...], up[...], 1, 0)
        sig = jax.nn.sigmoid(pre)
        hid_ref[...] = (pre * sig).astype(BF)
        dpre_ref[...] = (back_ref[...] * sig * (1.0 + pre * (1.0 - sig))).astype(BF)
        for c in copies:
            c.wait()
        packed_dx(dpre_ref, owned, dx_ref)

    half = pltpu.VMEM((HALF, HID), BF)
    return call(
        body,
        [SM, VM, VM, VM, HB],
        [((ROWS, HID), BF), ((ROWS, HID), BF), ((EXPERTS, CHIPS, PACK, LANES), BF)],
        [half, half, DMA((PARTS,)), DMA((2 * CHIPS,))],
        limit=TIGHT,
        flops=2 * ROWS * D * HID,
        nbytes=2 * D * HID,
    )(place, part, x_oth, back, panels)


def dx_mine(place, d_pre, panels):
    def body(place_ref, dpre_ref, panel_ref, dx_ref, owned, sems):
        for c in owned_rows(panel_ref, place_ref[0], owned, sems):
            c.wait()
        packed_dx(dpre_ref, owned, dx_ref)

    return call(
        body,
        [SM, VM, HB],
        [((EXPERTS, CHIPS, PACK, LANES), F32)],
        [pltpu.VMEM((HALF, HID), BF), DMA((2 * CHIPS,))],
        limit=TIGHT,
        flops=ROWS * D * HID,
        nbytes=D * HID,
    )(place, d_pre, panels)[0]


def weight_grads(place, own, oth, right, which, step, block, into=None):
    steps = HALF // step

    def body(place_ref, own_ref, oth_ref, right_ref, *rest):
        out_ref = rest[-1]
        k = pl.program_id(0)

        @pl.when(k < steps)
        def _():
            out_ref[0, 0] = matmul(own_ref[...], right_ref[...], 0, 0) * (1.0 / EXPERTS)

        @pl.when(k >= steps)
        def _():
            out_ref[0, 0] = matmul(oth_ref[...], right_ref[...], 0, 0) * (1.0 / EXPERTS)

    def target(k, p):
        side, k = k // steps, k % steps
        return (0, which, ((p[0] + side) % 2) * steps + block(k, p), 0)

    extra = [] if into is None else [into]
    return pl.pallas_call(
        body,
        grid_spec=pltpu.PrefetchScalarGridSpec(
            num_scalar_prefetch=1,
            grid=(2 * steps,),
            in_specs=[
                pl.BlockSpec((ROWS, step), lambda k, p: (0, jnp.minimum(k, steps - 1))),
                pl.BlockSpec((ROWS, step), lambda k, p: (0, jnp.clip(k - steps, 0, steps - 1))),
                pl.BlockSpec((ROWS, HID), lambda k, p: (0, 0)),
            ]
            + [ANY] * len(extra),
            out_specs=pl.BlockSpec((1, 1, step, HID), target),
        ),
        out_shape=jax.ShapeDtypeStruct((1, 2, D, HID), F32),
        input_output_aliases={4: 0} if extra else {},
        compiler_params=pltpu.CompilerParams(vmem_limit_bytes=20 * MIB),
        cost_estimate=pl.CostEstimate(
            flops=2 * ROWS * D * HID, transcendentals=0, bytes_accessed=4 * D * HID
        ),
    )(place, own, oth, right, *extra)


def combine(parts, hot):
    def body(parts_ref, hot_ref, out_ref):
        half = CAP // 2

        def summed(hots, rows):
            return matmul(rows.reshape(-1, LANES), hots.reshape(-1, TOK), 0, 0)

        hot = hot_ref[...].reshape(EXPERTS, 1, CAP, TOK)
        hot = jnp.broadcast_to(hot, (EXPERTS, CHIPS, CAP, TOK))
        parts = parts_ref[...].reshape(EXPERTS, CHIPS, PACK, LANES)
        packed = parts[:, :, CAP:, :]
        out_ref[:LANES, :] = summed(hot, parts[:, :, :CAP, :]).astype(BF)
        low = summed(hot[:, :, :half, :], packed)
        high = summed(hot[:, :, half:, :], packed)
        out_ref[LANES:, :] = (low[:REST, :] + high[REST:, :]).astype(BF)

    return call(body, [VM, VM], [((SLICE, TOK), BF)], [])(parts, hot)[0].T


def shards(tokens, expert_ids, gate_levels, out_grad, panels):
    core, x = lax.axis_index("core"), lax.axis_index("x")
    place = jnp.stack([core, x]).astype(jnp.int32)
    table = jnp.concatenate([expert_ids.T, gate_levels.T], axis=0)
    swap = [(0, 1), (1, 0)]

    def after(value, *deps):
        return lax.optimization_barrier((value,) + deps)[0]

    def exchange(rows, axes):
        return lax.all_to_all(rows, axes, split_axis=0, concat_axis=0, tiled=True)

    grad = lax.dynamic_slice(out_grad, (0, core * HALF + x * QUART), (TOK, QUART))
    d_small = dispatch_d(table, grad).reshape(EXPERTS, CAP, QUART)
    d_first = exchange(d_small, BLK).reshape(ROWS, QUART)
    tok = lax.dynamic_slice(after(tokens, d_small), (0, core * HALF), (TOK, HALF))
    x_rows, hot = dispatch_x(table, tok)
    x_sent = after(x_rows, d_first).reshape(EXPERTS, CAP, HALF)
    x_own = exchange(x_sent, BLK).reshape(ROWS, HALF)
    d_first = after(d_first, x_rows)
    d_own = assemble(
        [d_first]
        + [
            lax.ppermute(d_first, "x", [(i, (i + r) % XS) for i in range(XS)])
            for r in range(1, XS)
        ]
    )
    d_oth = lax.ppermute(d_own, "core", swap)
    back = back_full(place, d_own, d_oth, panels)
    x_oth = lax.ppermute(x_own, "core", swap)
    part = up_own(place, x_own, panels)
    hidden, d_pre, dx_send = middle(place, part, x_oth, back, panels)
    dx_recv = lax.ppermute(dx_send, "core", swap)
    chip_dx = (dx_mine(place, d_pre, panels) + dx_recv.astype(F32)).astype(BF)
    parts = exchange(chip_dx.reshape(DESTS, PACK, LANES), ("yhi", "z", "ylo", "x"))
    step = 512
    panel_grads = weight_grads(
        place, x_own, x_oth, after(d_pre, chip_dx), 0, step, lambda k, p: k
    )
    panel_grads = weight_grads(
        place, d_own, d_oth, hidden, 1, QUART, lambda k, p: (p[1] + XS - k) % XS, panel_grads
    )
    token_grad = combine(after(parts, panel_grads), hot)
    return token_grad, panel_grads


def solution(mesh):
    fine = Mesh(mesh.devices.reshape(SIZES), AXES)
    dp = AXES[:3]
    rows = P(BLK, None)
    return jax.shard_map(
        shards,
        mesh=fine,
        in_specs=(rows, rows, rows, rows, P(BLK, None, None, dp)),
        out_specs=(P(BLK, dp), P(BLK, None, None, dp)),
        check_vma=False,
    )
```

time: 304 us -> 116 us (0.38)
  waiting for transfers between devices: 165 us -> 34.4 us
  local copies, waits for them, and re-layouts: 55.7 us -> 4.71 us
  Pallas kernels: 0 us -> 44.9 us
  matrix products: 23.5 us -> 0 us
  other arithmetic: 27.3 us -> 4.98 us
  between operations: 14.2 us -> 0.8 us
  starting transfers between devices: 17.9 us -> 25.7 us
    all_to_all x3, waiting for transfers between devices: 121 us -> 16.7 us  [exchange(): return lax.all_to_all(rows, axes, split_axis=0, concat_axis=0, tiled=True)]
    pallas_call x0 -> x10, Pallas kernels: none -> 44.9 us  [the longest x2 14.5 us: weight_grads(): pl.pallas_call(body, grid_spec=pltpu.PrefetchScalarGridSpec(num_scalar_pr...]
    unnamed x2 -> x0, waiting for transfers between devices: 43.8 us -> none
    dot_general x5 -> x0, matrix products: 23.5 us -> none  [the longest x1 5.61 us: shards(): pre_act = jnp.dot(x_flat, w_up, preferred_element_type=jnp.float32)]
    scatter x2 -> x0, local copies, waits for them, and re-layouts: 22.4 us -> none  [the longest x1 11.2 us: slot_tables(): slot_gate = jnp.zeros((num_experts, capacity), jnp.float32).at[flat_ids,...]
    reshape x4 -> x0, local copies, waits for them, and re-layouts: 19.4 us -> none  [the longest x1 19 us: shards(): dx_part.reshape(1, cycle_len * capacity, model_dim)]
    ppermute x0 -> x6, waiting for transfers between devices: none -> 17.7 us  [the longest x3 17.7 us: shards(): lax.ppermute(d_first, 'x', [(i, (i + r) % XS) for i in range(XS)])]
    scatter-add x1 -> x0, other arithmetic: 12.8 us -> none  [gather_back(): summed = jnp.zeros((tok_count + 1, width), jnp.float32).at[slot_table.res...]
  transfers between devices with their start and end apart: 4 -> 9, of which waited for: 4 -> 4; matrix products, arithmetic and copies ran while one was open for 14% -> 1% of each run, Pallas kernels for 0% -> 29%
where the time goes in v2:
time: 116 us
  Pallas kernels  44.9 us (39%)
  waiting for transfers between devices  34.4 us (30%)
  starting transfers between devices  25.7 us (22%)
  other arithmetic  4.98 us (4%)
  local copies, waits for them, and re-layouts  4.71 us (4%)
    all_to_all x3, starting transfers between devices, exchange(): return lax.all_to_all(rows, axes, split_axis=0, concat_axis=0, tiled=True)  20.1 us
    ppermute x3, waiting for transfers between devices, shards(): lax.ppermute(d_first, 'x', [(i, (i + r) % XS) for i in range(XS)])  17.7 us
    all_to_all x3, waiting for transfers between devices, exchange(): return lax.all_to_all(rows, axes, split_axis=0, concat_axis=0, tiled=True)  16.7 us
    pallas_call x2, Pallas kernels, weight_grads(): pl.pallas_call(body, grid_spec=pltpu.PrefetchScalarGridSpec(num_scalar_pr...  14.5 us
    pallas_call x1, Pallas kernels, middle(): call(body, [SM, VM, VM, VM, HB], [((ROWS, HID), BF), ((ROWS, HID), BF), (...  7.6 us
    pallas_call x1, Pallas kernels, back_full(): call(body, [SM, VM, VM, HB], [((ROWS, HID), F32)], [pltpu.VMEM((D, HID),...  6.63 us
    pallas_call x1, Pallas kernels, dx_mine(): call(body, [SM, VM, HB], [((EXPERTS, CHIPS, PACK, LANES), F32)], [pltpu.V...  5.51 us
    pallas_call x1, Pallas kernels, up_own(): call(body, [SM, VM, HB], [((ROWS, HID), F32)], [pltpu.VMEM((HALF, HID), B...  4.75 us
  transfers between devices with their start and end apart: 9, of which 4 were waited for; matrix products, arithmetic and copies ran while one was open for 1% of the time, Pallas kernels for 29%

profile of v2, /device:TPU:0, one launch (start us, length us, event | category | flops | bytes accessed | tf_op | source)
XLA Modules:
  0.0 115.5 jit_solution(9442514150266604452)
XLA Ops:
  1.4 0.9 constant_dynamic-slice_fusion.1.grad_ref
  2.3 1.1 shard_map.68
  3.5 8.0 %all-to-all-start = ((bf16[8,64,384]{2,1,0:T(8,128)(2,1)}), bf16[8,64,384]{2,1,0:T(8,128)(2,1)S(1)}, u32[]{:S(2)}, u32[]{:S(2)}) async-start(bf16[8,64,384]{2,1,0:T(8,128)(2,1)} %bitcast.4), calls=%async_computation | async-start | bytes 786432 | tf_op jit(solution)/shard_map/all_to_all | solution.py:330
  12.3 1.1 copy-done.6
  13.4 8.1 %all-to-all-done = bf16[8,64,384]{2,1,0:T(8,128)(2,1)S(1)} async-done(((bf16[8,64,384]{2,1,0:T(8,128)(2,1)}), bf16[8,64,384]{2,1,0:T(8,128)(2,1)S(1)}, u32[]{:S(2)}, u32[]{:S(2)}) %all-to-all-start) | async-done | bytes 393248 | tf_op jit(solution)/shard_map/all_to_all | solution.py:330
  21.5 3.6 %all-to-all-start.1 = ((bf16[8,64,1536]{2,1,0:T(8,128)(2,1)}), bf16[8,64,1536]{2,1,0:T(8,128)(2,1)S(1)}, u32[]{:S(2)}, u32[]{:S(2)}) async-start(bf16[8,64,1536]{2,1,0:T(8,128)(2,1)} %bitcast.13), calls=%async_computation.1 | async-start | bytes 3145728 | tf_op jit(solution)/shard_map/all_to_all | solution.py:330
  25.0 2.8 %collective-permute-start.3 = (bf16[512,384]{1,0:T(8,128)(2,1)S(1)}, bf16[512,384]{1,0:T(8,128)(2,1)S(1)}, u32[]{:S(2)}, u32[]{:S(2)}) collective-permute-start(bf16[512,384]{1,0:T(8,128)(2,1)S(1)} %bitcast.14), channel_id=1, source_target_pairs={{0,48},{16,0},{32,16},{48,32},{1,49},{17,1},{33,17},{49,33},{2,50}... | collective-permute-start | bytes 1179656 | tf_op jit(solution)/shard_map/ppermute | solution.py:343
  27.9 0.8 collective-permute-start.2
  28.7 0.9 collective-permute-start.1
  29.6 14.0 %collective-permute-done.3.refs_3_ = bf16[512,384]{1,0:T(8,128)(2,1)S(1)} collective-permute-done((bf16[512,384]{1,0:T(8,128)(2,1)S(1)}, bf16[512,384]{1,0:T(8,128)(2,1)S(1)}, u32[]{:S(2)}, u32[]{:S(2)}) %collective-permute-start.3) | collective-permute-done | bytes 393248 | tf_op jit(solution)/shard_map/ppermute | solution.py:343
  43.6 3.7 %collective-permute-done.1.refs_1_ = bf16[512,384]{1,0:T(8,128)(2,1)S(1)} collective-permute-done((bf16[512,384]{1,0:T(8,128)(2,1)S(1)}, bf16[512,384]{1,0:T(8,128)(2,1)S(1)}, u32[]{:S(2)}, u32[]{:S(2)}) %collective-permute-start.1) | collective-permute-done | bytes 393248 | tf_op jit(solution)/shard_map/ppermute | solution.py:343
  47.3 1.3 %shard_map.71.own_ref = bf16[512,1536]{1,0:T(8,128)(2,1)} custom-call(bf16[512,384]{1,0:T(8,128)(2,1)S(1)} %bitcast.17, bf16[512,384]{1,0:T(8,128)(2,1)S(1)} %collective-permute-done.1.refs_1_, bf16[512,384]{1,0:T(8,128)(2,1)S(1)} %collective-permute-done.2.refs_2_, bf16[512,384]{1,0:T(8,128)(2,1)S(1)} %collective-permute-done.3.refs_3_), custom_call_target="tpu_custom_call" | custom-call | tf_op jit(solution)/shard_map/pallas_call | solution.py:110
  49.8 4.7 %shard_map.70.part_ref = f32[512,512]{1,0:T(8,128)} custom-call(s32[2]{0:T(128)} %pad_add_fusion.1.place_ref, bf16[512,1536]{1,0:T(8,128)(2,1)} %bitcast.11, bf16[1,2,3072,512]{3,2,1,0:T(8,128)(2,1)} %panel_ref.7), custom_call_target="tpu_custom_call" | custom-call | flops 805306368 | bytes 1572864 | tf_op jit(solution)/shard_map/pallas_call | solution.py:182
  54.5 6.6 %shard_map.72.back_ref = f32[512,512]{1,0:T(8,128)} custom-call(s32[2]{0:T(128)} %pad_add_fusion.1.place_ref, bf16[512,1536]{1,0:T(8,128)(2,1)} %shard_map.71.own_ref, bf16[512,1536]{1,0:T(8,128)(2,1)} %collective-permute-done.4.oth_ref, bf16[1,2,3072,512]{3,2,1,0:T(8,128)(2,1)} %panel_ref.7), custom_call_target="tpu_custom_call" | custom-call | flops 1610612736 | bytes 3145728 | tf_op jit(solution)/shard_map/pallas_call | solution.py:165
  61.2 1.2 %copy-done.3 = bf16[512,1536]{1,0:T(8,128)(2,1)} copy-done((bf16[512,1536]{1,0:T(8,128)(2,1)}, bf16[512,1536]{1,0:T(8,128)(2,1)S(1)}, u32[]{:S(2)}) %copy-start.3) | copy-done | bytes 1572888
  62.4 7.6 %shard_map.73 = (bf16[512,512]{1,0:T(8,128)(2,1)}, bf16[512,512]{1,0:T(8,128)(2,1)}, bf16[8,8,96,128]{3,2,1,0:T(8,128)(2,1)}) custom-call(s32[2]{0:T(128)} %pad_add_fusion.1.place_ref, f32[512,512]{1,0:T(8,128)} %shard_map.70.part_ref, bf16[512,1536]{1,0:T(8,128)(2,1)} %copy-done.3, f32[512,512]{1,0:T(8,128)} %shard_map.72.back_ref, ...), custom_call_target="tpu_custom_call" | custom-call | flops 1610612736 | bytes 3145728 | tf_op jit(solution)/shard_map/pallas_call | solution.py:231
  70.5 5.5 %shard_map.74 = f32[8,8,96,128]{3,2,1,0:T(8,128)} custom-call(s32[2]{0:T(128)} %pad_add_fusion.1.place_ref, bf16[512,512]{1,0:T(8,128)(2,1)} %get-tuple-element.19.dpre_ref.right_ref, bf16[1,2,3072,512]{3,2,1,0:T(8,128)(2,1)} %panel_ref.7), custom_call_target="tpu_custom_call" | custom-call | flops 805306368 | bytes 1572864 | tf_op jit(solution)/shard_map/pallas_call | solution.py:248
  76.1 3.6 %add_convert_fusion = bf16[8,8,96,128]{3,2,1,0:T(8,128)(2,1)} fusion(f32[8,8,96,128]{3,2,1,0:T(8,128)} %shard_map.74, bf16[8,8,96,128]{3,2,1,0:T(8,128)(2,1)S(1)} %collective-permute-done.5), kind=kLoop, calls=%fused_computation | loop fusion | flops 2359296 | bytes 6291456 | tf_op jit(solution)/shard_map/convert_element_type | solution.py:353
  79.6 8.5 %all-to-all-start.2 = ((bf16[64,96,128]{2,1,0:T(8,128)(2,1)}), bf16[64,96,128]{2,1,0:T(8,128)(2,1)}, u32[]{:S(2)}, u32[]{:S(2)}) async-start(bf16[64,96,128]{2,1,0:T(8,128)(2,1)} %bitcast.18), calls=%async_computation.2 | async-start | bytes 3145728 | tf_op jit(solution)/shard_map/all_to_all | solution.py:330
  88.2 1.4 %copy-done.4 = bf16[512,1536]{1,0:T(8,128)(2,1)S(1)} copy-done((bf16[512,1536]{1,0:T(8,128)(2,1)S(1)}, bf16[512,1536]{1,0:T(8,128)(2,1)}, u32[]{:S(2)}) %copy-start.4) | copy-done | bytes 1572888
  89.6 5.7 %shard_map.75.rest_0_ = f32[1,2,3072,512]{3,2,1,0:T(8,128)} custom-call(s32[2]{0:T(128)S(1)} %copy-done.8, bf16[512,1536]{1,0:T(8,128)(2,1)S(1)} %bitcast.12, bf16[512,1536]{1,0:T(8,128)(2,1)S(1)} %copy-done.4, bf16[512,512]{1,0:T(8,128)(2,1)S(1)} %copy-done.5), custom_call_target="tpu_custom_call" | custom-call | flops 1610612736 | bytes 6291456 | tf_op jit(solution)/shard_map/pallas_call | solution.py:279
  95.3 8.7 %shard_map.76 = f32[1,2,3072,512]{3,2,1,0:T(8,128)} custom-call(s32[2]{0:T(128)S(1)} %copy-done.8, bf16[512,1536]{1,0:T(8,128)(2,1)} %shard_map.71.own_ref, bf16[512,1536]{1,0:T(8,128)(2,1)} %collective-permute-done.4.oth_ref, bf16[512,512]{1,0:T(8,128)(2,1)S(1)} %copy-done.7, f32[1,2,3072,512]{3,2,1,0:T(8,128)} %shard_map.75.rest_0_), custom_call_target="tpu_custom_call", output_to_operand_aliasing={{}: (4, {})} | custom-call | flops 1610612736 | bytes 6291456 | tf_op jit(solution)/shard_map/pallas_call | solution.py:279
  104.1 8.7 %all-to-all-done.2.parts_ref = bf16[64,96,128]{2,1,0:T(8,128)(2,1)} async-done(((bf16[64,96,128]{2,1,0:T(8,128)(2,1)}), bf16[64,96,128]{2,1,0:T(8,128)(2,1)}, u32[]{:S(2)}, u32[]{:S(2)}) %all-to-all-start.2) | async-done | bytes 1572896 | tf_op jit(solution)/shard_map/all_to_all | solution.py:330
  112.7 2.8 %shard_map.77 = bf16[192,128]{1,0:T(8,128)(2,1)} custom-call(bf16[64,96,128]{2,1,0:T(8,128)(2,1)} %all-to-all-done.2.parts_ref, bf16[512,128]{1,0:T(8,128)(2,1)S(1)} %get-tuple-element.21.hot_ref), custom_call_target="tpu_custom_call" | custom-call | tf_op jit(solution)/shard_map/pallas_call | solution.py:317
  (27 shorter events, 3.3 us)
Async XLA Ops:
  0.6 10.9 %copy-start = (bf16[128,3072]{1,0:T(8,128)(2,1)S(1)}, bf16[128,3072]{1,0:T(8,128)(2,1)}, u32[]{:S(2)}) copy-start(bf16[128,3072]{1,0:T(8,128)(2,1)} %param.5) | copy-start | bytes 2359300
  3.5 18.0 %all-to-all-start = ((bf16[8,64,384]{2,1,0:T(8,128)(2,1)}), bf16[8,64,384]{2,1,0:T(8,128)(2,1)S(1)}, u32[]{:S(2)}, u32[]{:S(2)}) async-start(bf16[8,64,384]{2,1,0:T(8,128)(2,1)} %bitcast.4), calls=%async_computation | async-start | bytes 786432 | tf_op jit(solution)/shard_map/all_to_all | solution.py:330
  12.3 1.1 copy-start.6
  21.5 27.1 %all-to-all-start.1 = ((bf16[8,64,1536]{2,1,0:T(8,128)(2,1)}), bf16[8,64,1536]{2,1,0:T(8,128)(2,1)S(1)}, u32[]{:S(2)}, u32[]{:S(2)}) async-start(bf16[8,64,1536]{2,1,0:T(8,128)(2,1)} %bitcast.13), calls=%async_computation.1 | async-start | bytes 3145728 | tf_op jit(solution)/shard_map/all_to_all | solution.py:330
  25.0 18.5 %collective-permute-start.3 = (bf16[512,384]{1,0:T(8,128)(2,1)S(1)}, bf16[512,384]{1,0:T(8,128)(2,1)S(1)}, u32[]{:S(2)}, u32[]{:S(2)}) collective-permute-start(bf16[512,384]{1,0:T(8,128)(2,1)S(1)} %bitcast.14), channel_id=1, source_target_pairs={{0,48},{16,0},{32,16},{48,32},{1,49},{17,1},{33,17},{49,33},{2,50}... | collective-permute-start | bytes 1179656 | tf_op jit(solution)/shard_map/ppermute | solution.py:343
  27.9 15.7 %collective-permute-start.2 = (bf16[512,384]{1,0:T(8,128)(2,1)S(1)}, bf16[512,384]{1,0:T(8,128)(2,1)S(1)}, u32[]{:S(2)}, u32[]{:S(2)}) collective-permute-start(bf16[512,384]{1,0:T(8,128)(2,1)S(1)} %bitcast.15), channel_id=1, source_target_pairs={{0,32},{16,48},{32,0},{48,16},{1,33},{17,49},{33,1},{49,17},{2,34}... | collective-permute-start | bytes 1179656 | tf_op jit(solution)/shard_map/ppermute | solution.py:343
  28.7 18.6 %collective-permute-start.1 = (bf16[512,384]{1,0:T(8,128)(2,1)S(1)}, bf16[512,384]{1,0:T(8,128)(2,1)S(1)}, u32[]{:S(2)}, u32[]{:S(2)}) collective-permute-start(bf16[512,384]{1,0:T(8,128)(2,1)S(1)} %bitcast.16), channel_id=1, source_target_pairs={{0,16},{16,32},{32,48},{48,0},{1,17},{17,33},{33,49},{49,1},{2,18}... | collective-permute-start | bytes 1179656 | tf_op jit(solution)/shard_map/ppermute | solution.py:343
  48.6 5.9 %collective-permute-start.4 = (bf16[512,1536]{1,0:T(8,128)(2,1)}, bf16[512,1536]{1,0:T(8,128)(2,1)}, u32[]{:S(2)}, u32[]{:S(2)}) collective-permute-start(bf16[512,1536]{1,0:T(8,128)(2,1)} %shard_map.71.own_ref), channel_id=1, source_target_pairs={{0,8},{8,0},{1,9},{9,1},{2,10},{10,2},{3,11},{11,3},{4,12},{12,4},... | collective-permute-start | bytes 4718600 | tf_op jit(solution)/shard_map/ppermute | solution.py:347
  48.6 1.2 %copy-start.1 = (bf16[8,64,1536]{2,1,0:T(8,128)(2,1)}, bf16[8,64,1536]{2,1,0:T(8,128)(2,1)S(1)}, u32[]{:S(2)}) copy-start(bf16[8,64,1536]{2,1,0:T(8,128)(2,1)S(1)} %all-to-all-done.1) | copy-start | bytes 4718596
  48.6 12.6 %collective-permute-start = (bf16[512,1536]{1,0:T(8,128)(2,1)S(1)}, bf16[512,1536]{1,0:T(8,128)(2,1)S(1)}, u32[]{:S(2)}, u32[]{:S(2)}) collective-permute-start(bf16[512,1536]{1,0:T(8,128)(2,1)S(1)} %bitcast.10), channel_id=1, source_target_pairs={{0,8},{8,0},{1,9},{9,1},{2,10},{10,2},{3,11},{11,3},{4,12},{12,4},... | collective-permute-start | bytes 4718600 | tf_op jit(solution)/shard_map/ppermute | solution.py:349
  61.2 1.2 %copy-start.3 = (bf16[512,1536]{1,0:T(8,128)(2,1)}, bf16[512,1536]{1,0:T(8,128)(2,1)S(1)}, u32[]{:S(2)}) copy-start(bf16[512,1536]{1,0:T(8,128)(2,1)S(1)} %collective-permute-done.oth_ref) | copy-start | bytes 4718596
  70.0 6.1 %collective-permute-start.5 = (bf16[8,8,96,128]{3,2,1,0:T(8,128)(2,1)}, bf16[8,8,96,128]{3,2,1,0:T(8,128)(2,1)S(1)}, u32[]{:S(2)}, u32[]{:S(2)}) collective-permute-start(bf16[8,8,96,128]{3,2,1,0:T(8,128)(2,1)} %get-tuple-element.17), channel_id=1, source_target_pairs={{0,8},{8,0},{1,9},{9,1},{2,10},{10,2},{3,11},{11,3},{4,12},{12,4},... | collective-permute-start | bytes 4718600 | tf_op jit(solution)/shard_map/ppermute | solution.py:352
  79.6 8.5 %copy-start.2 = (bf16[8,64,1536]{2,1,0:T(8,128)(2,1)S(1)}, bf16[8,64,1536]{2,1,0:T(8,128)(2,1)}, u32[]{:S(2)}) copy-start(bf16[8,64,1536]{2,1,0:T(8,128)(2,1)} %copy-done.1) | copy-start | bytes 4718596
  79.6 8.6 %copy-start.5 = (bf16[512,512]{1,0:T(8,128)(2,1)S(1)}, bf16[512,512]{1,0:T(8,128)(2,1)}, u32[]{:S(2)}) copy-start(bf16[512,512]{1,0:T(8,128)(2,1)} %get-tuple-element.19.dpre_ref.right_ref) | copy-start | bytes 1572868
  79.6 8.6 %copy-start.8 = (s32[2]{0:T(128)S(1)}, s32[2]{0:T(128)}, u32[]{:S(2)}) copy-start(s32[2]{0:T(128)} %pad_add_fusion.1.place_ref) | copy-start | bytes 28
  79.6 33.1 %all-to-all-start.2 = ((bf16[64,96,128]{2,1,0:T(8,128)(2,1)}), bf16[64,96,128]{2,1,0:T(8,128)(2,1)}, u32[]{:S(2)}, u32[]{:S(2)}) async-start(bf16[64,96,128]{2,1,0:T(8,128)(2,1)} %bitcast.18), calls=%async_computation.2 | async-start | bytes 3145728 | tf_op jit(solution)/shard_map/all_to_all | solution.py:330
  88.2 1.4 %copy-start.4 = (bf16[512,1536]{1,0:T(8,128)(2,1)S(1)}, bf16[512,1536]{1,0:T(8,128)(2,1)}, u32[]{:S(2)}) copy-start(bf16[512,1536]{1,0:T(8,128)(2,1)} %copy-done.3) | copy-start | bytes 4718596
  89.6 5.7 %copy-start.7 = (bf16[512,512]{1,0:T(8,128)(2,1)S(1)}, bf16[512,512]{1,0:T(8,128)(2,1)}, u32[]{:S(2)}) copy-start(bf16[512,512]{1,0:T(8,128)(2,1)} %get-tuple-element.18.right_ref) | copy-start | bytes 1572868

commit v3 on v2

--- a/solution.py
+++ b/solution.py
@@ -102,91 +102,50 @@
     )(table, out_grad)[0]
 
 
-def assemble(pieces):
-    def body(*refs):
+def assemble(place, pieces):
+    def body(place_ref, *refs):
         for r in range(XS):
-            refs[XS][:, r * QUART : (r + 1) * QUART] = refs[r][...]
-
-    return call(body, [VM] * XS, [((ROWS, HALF), BF)], [])(*pieces)[0]
-
-
-TIGHT = 59
-
-
-def panel_rows(panel_ref, which, start, unit, count, buf, into, sem):
-    rows = pl.ds(pl.multiple_of(start, unit), count)
-    copy = pltpu.make_async_copy(panel_ref.at[0, which, rows, :], buf.at[pl.ds(into, count), :], sem)
-    copy.start()
-    return copy
-
-
-def owned_rows(panel_ref, o, buf, sems):
-    copies = []
+            start = ((place_ref[1] + XS - r) % XS) * QUART
+            refs[XS][:, pl.ds(pl.multiple_of(start, LANES), QUART)] = refs[r][...]
+
+    return call(body, [SM] + [VM] * XS, [((ROWS, HALF), BF)], [])(place, *pieces)[0]
+
+
+def half_of(panel_ref, which, half):
+    return panel_ref[0, which, pl.ds(pl.multiple_of(half * HALF, HALF), HALF), :]
+
+
+def owned_rows(panel_ref, o, buf):
     for j in range(CHIPS):
-        first = (2 * j + o) * SLICE
-        copies.append(panel_rows(panel_ref, 0, first, 64, LANES, buf, j * LANES, sems.at[2 * j]))
-        copies.append(
-            panel_rows(
-                panel_ref, 0, first + LANES, 64, REST, buf, CHIPS * LANES + j * REST, sems.at[2 * j + 1]
-            )
-        )
-    return copies
-
-
-PARTS = 3
-PART = HALF // PARTS
-
-
-def half_rows(panel_ref, o, buf, sems):
-    return [
-        panel_rows(panel_ref, 0, o * HALF + i * PART, PART, PART, buf, i * PART, sems.at[i])
-        for i in range(PARTS)
-    ]
+        first = pl.multiple_of((2 * j + o) * SLICE, SLICE)
+        into = CHIPS * LANES + j * REST
+        buf[j * LANES : (j + 1) * LANES, :] = panel_ref[0, 0, pl.ds(first, LANES), :]
+        rest = pl.multiple_of(first + LANES, REST)
+        buf[into : into + REST, :] = panel_ref[0, 0, pl.ds(rest, REST), :]
 
 
 def back_full(place, d_own, d_oth, panels):
-    def body(place_ref, own_ref, oth_ref, panel_ref, out_ref, buf, sems):
-        copies = []
-        for side in range(2):
-            o = (place_ref[0] + side) % 2
-            for r in range(XS):
-                start = (o * XS + (place_ref[1] + XS - r) % XS) * QUART
-                i = side * XS + r
-                copies.append(
-                    panel_rows(panel_ref, 1, start, QUART, QUART, buf, i * QUART, sems.at[i])
-                )
-        for c in copies[:XS]:
-            c.wait()
-        own = matmul(own_ref[...], buf[:HALF, :], 1, 0)
-        for c in copies[XS:]:
-            c.wait()
-        out_ref[...] = own + matmul(oth_ref[...], buf[HALF:, :], 1, 0)
-
-    return call(
-        body,
-        [SM, VM, VM, HB],
+    def body(place_ref, own_ref, oth_ref, panel_ref, out_ref):
+        core = place_ref[0]
+        own = matmul(own_ref[...], half_of(panel_ref, 1, core), 1, 0)
+        out_ref[...] = own + matmul(oth_ref[...], half_of(panel_ref, 1, 1 - core), 1, 0)
+
+    return call(
+        body,
+        [SM, VM, VM, VM],
         [((ROWS, HID), F32)],
-        [pltpu.VMEM((D, HID), BF), DMA((2 * XS,))],
-        limit=TIGHT,
+        [],
         flops=2 * ROWS * D * HID,
         nbytes=2 * D * HID,
     )(place, d_own, d_oth, panels)[0]
 
 
 def up_own(place, x_own, panels):
-    def body(place_ref, own_ref, panel_ref, out_ref, buf, sems):
-        for c in half_rows(panel_ref, place_ref[0], buf, sems):
-            c.wait()
-        out_ref[...] = matmul(own_ref[...], buf[...], 1, 0)
-
-    return call(
-        body,
-        [SM, VM, HB],
-        [((ROWS, HID), F32)],
-        [pltpu.VMEM((HALF, HID), BF), DMA((PARTS,))],
-        limit=TIGHT,
-        flops=ROWS * D * HID,
-        nbytes=D * HID,
+    def body(place_ref, own_ref, panel_ref, out_ref):
+        out_ref[...] = matmul(own_ref[...], half_of(panel_ref, 0, place_ref[0]), 1, 0)
+
+    return call(
+        body, [SM, VM, VM], [((ROWS, HID), F32)], [], flops=ROWS * D * HID, nbytes=D * HID
     )(place, x_own, panels)[0]
 
 
@@ -212,51 +171,42 @@
 
 
 def middle(place, part, x_oth, back, panels):
-    def body(place_ref, part_ref, oth_ref, back_ref, panel_ref, hid_ref, dpre_ref, dx_ref, *tmp):
-        up, owned, up_sems, sems = tmp
+    def body(place_ref, part_ref, oth_ref, back_ref, panel_ref, hid_ref, dpre_ref, dx_ref, owned):
         other = 1 - place_ref[0]
-        ups = half_rows(panel_ref, other, up, up_sems)
-        copies = owned_rows(panel_ref, other, owned, sems)
-        for c in ups:
-            c.wait()
-        pre = part_ref[...] + matmul(oth_ref[...], up[...], 1, 0)
+        pre = part_ref[...] + matmul(oth_ref[...], half_of(panel_ref, 0, other), 1, 0)
+        owned_rows(panel_ref, other, owned)
         sig = jax.nn.sigmoid(pre)
         hid_ref[...] = (pre * sig).astype(BF)
         dpre_ref[...] = (back_ref[...] * sig * (1.0 + pre * (1.0 - sig))).astype(BF)
-        for c in copies:
-            c.wait()
         packed_dx(dpre_ref, owned, dx_ref)
 
-    half = pltpu.VMEM((HALF, HID), BF)
-    return call(
-        body,
-        [SM, VM, VM, VM, HB],
+    return call(
+        body,
+        [SM, VM, VM, VM, VM],
         [((ROWS, HID), BF), ((ROWS, HID), BF), ((EXPERTS, CHIPS, PACK, LANES), BF)],
-        [half, half, DMA((PARTS,)), DMA((2 * CHIPS,))],
-        limit=TIGHT,
+        [pltpu.VMEM((HALF, HID), BF)],
         flops=2 * ROWS * D * HID,
         nbytes=2 * D * HID,
     )(place, part, x_oth, back, panels)
 
 
 def dx_mine(place, d_pre, panels):
-    def body(place_ref, dpre_ref, panel_ref, dx_ref, owned, sems):
-        for c in owned_rows(panel_ref, place_ref[0], owned, sems):
-            c.wait()
+    def body(place_ref, dpre_ref, panel_ref, dx_ref, owned):
+        owned_rows(panel_ref, place_ref[0], owned)
         packed_dx(dpre_ref, owned, dx_ref)
 
     return call(
         body,
-        [SM, VM, HB],
+        [SM, VM, VM],
         [((EXPERTS, CHIPS, PACK, LANES), F32)],
-        [pltpu.VMEM((HALF, HID), BF), DMA((2 * CHIPS,))],
-        limit=TIGHT,
+        [pltpu.VMEM((HALF, HID), BF)],
         flops=ROWS * D * HID,
         nbytes=D * HID,
     )(place, d_pre, panels)[0]
 
 
-def weight_grads(place, own, oth, right, which, step, block, into=None):
+def weight_grads(place, own, oth, right, which, into=None):
+    step = 512
     steps = HALF // step
 
     def body(place_ref, own_ref, oth_ref, right_ref, *rest):
@@ -273,7 +223,7 @@
 
     def target(k, p):
         side, k = k // steps, k % steps
-        return (0, which, ((p[0] + side) % 2) * steps + block(k, p), 0)
+        return (0, which, ((p[0] + side) % 2) * steps + k, 0)
 
     extra = [] if into is None else [into]
     return pl.pallas_call(
@@ -338,11 +288,12 @@
     x_own = exchange(x_sent, BLK).reshape(ROWS, HALF)
     d_first = after(d_first, x_rows)
     d_own = assemble(
+        place,
         [d_first]
         + [
             lax.ppermute(d_first, "x", [(i, (i + r) % XS) for i in range(XS)])
             for r in range(1, XS)
-        ]
+        ],
     )
     d_oth = lax.ppermute(d_own, "core", swap)
     back = back_full(place, d_own, d_oth, panels)
@@ -352,13 +303,8 @@
     dx_recv = lax.ppermute(dx_send, "core", swap)
     chip_dx = (dx_mine(place, d_pre, panels) + dx_recv.astype(F32)).astype(BF)
     parts = exchange(chip_dx.reshape(DESTS, PACK, LANES), ("yhi", "z", "ylo", "x"))
-    step = 512
-    panel_grads = weight_grads(
-        place, x_own, x_oth, after(d_pre, chip_dx), 0, step, lambda k, p: k
-    )
-    panel_grads = weight_grads(
-        place, d_own, d_oth, hidden, 1, QUART, lambda k, p: (p[1] + XS - k) % XS, panel_grads
-    )
+    panel_grads = weight_grads(place, x_own, x_oth, after(d_pre, chip_dx), 0)
+    panel_grads = weight_grads(place, d_own, d_oth, hidden, 1, panel_grads)
     token_grad = combine(after(parts, panel_grads), hot)
     return token_grad, panel_grads
 

time: 116 us -> 103 us (0.89)
  Pallas kernels: 44.9 us -> 29.5 us
  waiting for transfers between devices: 34.4 us -> 38.1 us
  other arithmetic: 4.98 us -> 2.49 us
  local copies, waits for them, and re-layouts: 4.71 us -> 6.57 us
    pallas_call x5, Pallas kernels: 25.8 us -> 11.5 us  [the longest x1 3.68 us: back_full(): call(body, [SM, VM, VM, VM], [((ROWS, HID), F32)], [], flops=2 * ROWS * D...]
    convert_element_type x1, other arithmetic: 3.57 us -> 1.64 us  [shards(): chip_dx = (dx_mine(place, d_pre, panels) + dx_recv.astype(F32)).astype(BF)]
    unnamed x18 -> x12, local copies, waits for them, and re-layouts: 3.78 us -> 5.64 us
    ppermute x1, waiting for transfers between devices: 0.01 us -> 1.61 us  [shards(): dx_recv = lax.ppermute(dx_send, 'core', swap)]
    all_to_all x3, waiting for transfers between devices: 16.7 us -> 17.9 us  [exchange(): return lax.all_to_all(rows, axes, split_axis=0, concat_axis=0, tiled=True)]
  transfers between devices with their start and end apart: 9 -> 9, of which waited for: 4 -> 6; matrix products, arithmetic and copies ran while one was open for 1% -> 0% of each run, Pallas kernels for 29% -> 22%
where the time goes in v3:
time: 103 us
  waiting for transfers between devices  38.1 us (37%)
  Pallas kernels  29.5 us (29%)
  starting transfers between devices  25.1 us (24%)
  local copies, waits for them, and re-layouts  6.57 us (6%)
  other arithmetic  2.49 us (2%)
    all_to_all x3, starting transfers between devices, exchange(): return lax.all_to_all(rows, axes, split_axis=0, concat_axis=0, tiled=True)  20 us
    all_to_all x3, waiting for transfers between devices, exchange(): return lax.all_to_all(rows, axes, split_axis=0, concat_axis=0, tiled=True)  17.9 us
    ppermute x3, waiting for transfers between devices, shards(): lax.ppermute(d_first, 'x', [(i, (i + r) % XS) for i in range(XS)])  17.6 us
    pallas_call x2, Pallas kernels, weight_grads(): pl.pallas_call(body, grid_spec=pltpu.PrefetchScalarGridSpec(num_scalar_pr...  13.4 us
    unnamed x12, local copies, waits for them, and re-layouts  5.64 us
    ppermute x3, starting transfers between devices, shards(): lax.ppermute(d_first, 'x', [(i, (i + r) % XS) for i in range(XS)])  4.51 us
    pallas_call x1, Pallas kernels, back_full(): call(body, [SM, VM, VM, VM], [((ROWS, HID), F32)], [], flops=2 * ROWS * D...  3.68 us
    pallas_call x1, Pallas kernels, combine(): return call(body, [VM, VM], [((SLICE, TOK), BF)], [])(parts, hot)[0].T  2.78 us
  transfers between devices with their start and end apart: 9, of which 6 were waited for; matrix products, arithmetic and copies ran while one was open for 0% of the time, Pallas kernels for 22%

profile of v3, /device:TPU:0, one launch (start us, length us, event | category | flops | bytes accessed | tf_op | source)
XLA Modules:
  0.0 102.6 jit_solution(17775132044774758786)
XLA Ops:
  1.4 0.9 constant_dynamic-slice_fusion.1.grad_ref
  2.3 1.1 %shard_map.68 = bf16[512,384]{1,0:T(8,128)(2,1)} custom-call(s32[4,128]{1,0:T(4,128)S(1)} %pad_add_fusion.table_ref, bf16[128,384]{1,0:T(8,128)(2,1)S(1)} %constant_dynamic-slice_fusion.1.grad_ref), custom_call_target="tpu_custom_call" | custom-call | tf_op jit(solution)/shard_map/pallas_call | solution.py:97
  3.5 8.0 %all-to-all-start = ((bf16[8,64,384]{2,1,0:T(8,128)(2,1)}), bf16[8,64,384]{2,1,0:T(8,128)(2,1)S(1)}, u32[]{:S(2)}, u32[]{:S(2)}) async-start(bf16[8,64,384]{2,1,0:T(8,128)(2,1)} %bitcast.4), calls=%async_computation | async-start | bytes 786432 | tf_op jit(solution)/shard_map/all_to_all | solution.py:280
  12.3 1.1 %copy-done.5 = bf16[512,1536]{1,0:T(8,128)(2,1)} copy-done((bf16[512,1536]{1,0:T(8,128)(2,1)}, bf16[512,1536]{1,0:T(8,128)(2,1)S(1)}, u32[]{:S(2)}) %copy-start.5) | copy-done | bytes 1572888
  13.4 8.1 %all-to-all-done = bf16[8,64,384]{2,1,0:T(8,128)(2,1)S(1)} async-done(((bf16[8,64,384]{2,1,0:T(8,128)(2,1)}), bf16[8,64,384]{2,1,0:T(8,128)(2,1)S(1)}, u32[]{:S(2)}, u32[]{:S(2)}) %all-to-all-start) | async-done | bytes 393248 | tf_op jit(solution)/shard_map/all_to_all | solution.py:280
  21.4 3.6 %all-to-all-start.1 = ((bf16[8,64,1536]{2,1,0:T(8,128)(2,1)}), bf16[8,64,1536]{2,1,0:T(8,128)(2,1)S(1)}, u32[]{:S(2)}, u32[]{:S(2)}) async-start(bf16[8,64,1536]{2,1,0:T(8,128)(2,1)} %bitcast.13), calls=%async_computation.1 | async-start | bytes 3145728 | tf_op jit(solution)/shard_map/all_to_all | solution.py:280
  25.0 2.8 %collective-permute-start.3 = (bf16[512,384]{1,0:T(8,128)(2,1)S(1)}, bf16[512,384]{1,0:T(8,128)(2,1)S(1)}, u32[]{:S(2)}, u32[]{:S(2)}) collective-permute-start(bf16[512,384]{1,0:T(8,128)(2,1)S(1)} %bitcast.14), channel_id=1, source_target_pairs={{0,48},{16,0},{32,16},{48,32},{1,49},{17,1},{33,17},{49,33},{2,50}... | collective-permute-start | bytes 1179656 | tf_op jit(solution)/shard_map/ppermute | solution.py:294
  29.6 14.0 %collective-permute-done.3.refs_3_ = bf16[512,384]{1,0:T(8,128)(2,1)S(1)} collective-permute-done((bf16[512,384]{1,0:T(8,128)(2,1)S(1)}, bf16[512,384]{1,0:T(8,128)(2,1)S(1)}, u32[]{:S(2)}, u32[]{:S(2)}) %collective-permute-start.3) | collective-permute-done | bytes 393248 | tf_op jit(solution)/shard_map/ppermute | solution.py:294
  43.6 3.7 %collective-permute-done.1.refs_1_ = bf16[512,384]{1,0:T(8,128)(2,1)S(1)} collective-permute-done((bf16[512,384]{1,0:T(8,128)(2,1)S(1)}, bf16[512,384]{1,0:T(8,128)(2,1)S(1)}, u32[]{:S(2)}, u32[]{:S(2)}) %collective-permute-start.1) | collective-permute-done | bytes 393248 | tf_op jit(solution)/shard_map/ppermute | solution.py:294
  47.3 1.8 %shard_map.71.own_ref = bf16[512,1536]{1,0:T(8,128)(2,1)} custom-call(s32[2]{0:T(128)S(1)} %pad_add_fusion.1.place_ref, bf16[512,384]{1,0:T(8,128)(2,1)S(1)} %bitcast.17, bf16[512,384]{1,0:T(8,128)(2,1)S(1)} %collective-permute-done.1.refs_1_, bf16[512,384]{1,0:T(8,128)(2,1)S(1)} %collective-permute-done.2.refs_2_, ...), custom_call_target="tpu_custom_call" | custom-call | tf_op jit(solution)/shard_map/pallas_call | solution.py:111
  49.6 2.8 %copy-done.1 = bf16[1,2,3072,512]{3,2,1,0:T(8,128)(2,1)S(1)} copy-done((bf16[1,2,3072,512]{3,2,1,0:T(8,128)(2,1)S(1)}, bf16[1,2,3072,512]{3,2,1,0:T(8,128)(2,1)}, u32[]{:S(2)}) %copy-start.1) | copy-done | bytes 6291480
  52.4 1.5 %shard_map.70.part_ref = f32[512,512]{1,0:T(8,128)S(1)} custom-call(s32[2]{0:T(128)S(1)} %pad_add_fusion.1.place_ref, bf16[512,1536]{1,0:T(8,128)(2,1)S(1)} %bitcast.11, bf16[1,2,3072,512]{3,2,1,0:T(8,128)(2,1)S(1)} %copy-done.1), custom_call_target="tpu_custom_call" | custom-call | flops 805306368 | bytes 1572864 | tf_op jit(solution)/shard_map/pallas_call | solution.py:147
  53.9 1.0 collective-permute-done.4.oth_ref
  55.2 3.7 %shard_map.72.back_ref = f32[512,512]{1,0:T(8,128)S(1)} custom-call(s32[2]{0:T(128)S(1)} %pad_add_fusion.1.place_ref, bf16[512,1536]{1,0:T(8,128)(2,1)} %shard_map.71.own_ref, bf16[512,1536]{1,0:T(8,128)(2,1)} %collective-permute-done.4.oth_ref, bf16[1,2,3072,512]{3,2,1,0:T(8,128)(2,1)S(1)} %copy-done.2), custom_call_target="tpu_custom_call" | custom-call | flops 1610612736 | bytes 3145728 | tf_op jit(solution)/shard_map/pallas_call | solution.py:133
  58.9 2.7 %shard_map.73 = (bf16[512,512]{1,0:T(8,128)(2,1)S(1)}, bf16[512,512]{1,0:T(8,128)(2,1)S(1)}, bf16[8,8,96,128]{3,2,1,0:T(8,128)(2,1)S(1)}) custom-call(s32[2]{0:T(128)S(1)} %pad_add_fusion.1.place_ref, f32[512,512]{1,0:T(8,128)S(1)} %shard_map.70.part_ref, bf16[512,1536]{1,0:T(8,128)(2,1)S(1)} %collective-permute-done.oth_ref, ...), custom_call_target="tpu_custom_call" | custom-call | flops 1610612736 | bytes 3145728 | tf_op jit(solution)/shard_map/pallas_call | solution.py:183
  61.7 1.8 %shard_map.74 = f32[8,8,96,128]{3,2,1,0:T(8,128)S(1)} custom-call(s32[2]{0:T(128)S(1)} %pad_add_fusion.1.place_ref, bf16[512,512]{1,0:T(8,128)(2,1)S(1)} %get-tuple-element.19.dpre_ref.right_ref, bf16[1,2,3072,512]{3,2,1,0:T(8,128)(2,1)S(1)} %copy-done.2), custom_call_target="tpu_custom_call" | custom-call | flops 805306368 | bytes 1572864 | tf_op jit(solution)/shard_map/pallas_call | solution.py:198
  63.5 1.6 %collective-permute-done.5 = bf16[8,8,96,128]{3,2,1,0:T(8,128)(2,1)S(1)} collective-permute-done((bf16[8,8,96,128]{3,2,1,0:T(8,128)(2,1)S(1)}, bf16[8,8,96,128]{3,2,1,0:T(8,128)(2,1)S(1)}, u32[]{:S(2)}, u32[]{:S(2)}) %collective-permute-start.5) | collective-permute-done | bytes 1572896 | tf_op jit(solution)/shard_map/ppermute | solution.py:303
  65.1 1.6 %add_convert_fusion = bf16[8,8,96,128]{3,2,1,0:T(8,128)(2,1)} fusion(f32[8,8,96,128]{3,2,1,0:T(8,128)S(1)} %shard_map.74, bf16[8,8,96,128]{3,2,1,0:T(8,128)(2,1)S(1)} %collective-permute-done.5), kind=kLoop, calls=%fused_computation | loop fusion | flops 2359296 | bytes 6291456 | tf_op jit(solution)/shard_map/convert_element_type | solution.py:304
  66.7 8.4 %all-to-all-start.2 = ((bf16[64,96,128]{2,1,0:T(8,128)(2,1)}), bf16[64,96,128]{2,1,0:T(8,128)(2,1)}, u32[]{:S(2)}, u32[]{:S(2)}) async-start(bf16[64,96,128]{2,1,0:T(8,128)(2,1)} %bitcast.18), calls=%async_computation.2 | async-start | bytes 3145728 | tf_op jit(solution)/shard_map/all_to_all | solution.py:280
  75.1 1.4 %copy-done.4 = bf16[512,1536]{1,0:T(8,128)(2,1)S(1)} copy-done((bf16[512,1536]{1,0:T(8,128)(2,1)S(1)}, bf16[512,1536]{1,0:T(8,128)(2,1)}, u32[]{:S(2)}) %copy-start.4) | copy-done | bytes 1572888
  76.5 5.7 %shard_map.75.rest_0_ = f32[1,2,3072,512]{3,2,1,0:T(8,128)} custom-call(s32[2]{0:T(128)S(1)} %pad_add_fusion.1.place_ref, bf16[512,1536]{1,0:T(8,128)(2,1)S(1)} %bitcast.12, bf16[512,1536]{1,0:T(8,128)(2,1)S(1)} %copy-done.4, bf16[512,512]{1,0:T(8,128)(2,1)S(1)} %get-tuple-element.19.dpre_ref.right_ref), custom_call_target="tpu_custom_call" | custom-call | flops 1610612736 | bytes 6291456 | tf_op jit(solution)/shard_map/pallas_call | solution.py:229
  82.3 7.7 %shard_map.76 = f32[1,2,3072,512]{3,2,1,0:T(8,128)} custom-call(s32[2]{0:T(128)S(1)} %pad_add_fusion.1.place_ref, bf16[512,1536]{1,0:T(8,128)(2,1)} %shard_map.71.own_ref, bf16[512,1536]{1,0:T(8,128)(2,1)} %collective-permute-done.4.oth_ref, bf16[512,512]{1,0:T(8,128)(2,1)S(1)} %get-tuple-element.18.right_ref, ...), custom_call_target="tpu_custom_call", output_to_operand_aliasing={{}: (4, {})} | custom-call | flops 1610612736 | bytes 6291456 | tf_op jit(solution)/shard_map/pallas_call | solution.py:229
  90.0 9.8 %all-to-all-done.2.parts_ref = bf16[64,96,128]{2,1,0:T(8,128)(2,1)} async-done(((bf16[64,96,128]{2,1,0:T(8,128)(2,1)}), bf16[64,96,128]{2,1,0:T(8,128)(2,1)}, u32[]{:S(2)}, u32[]{:S(2)}) %all-to-all-start.2) | async-done | bytes 1572896 | tf_op jit(solution)/shard_map/all_to_all | solution.py:280
  99.8 2.8 %shard_map.77 = bf16[192,128]{1,0:T(8,128)(2,1)} custom-call(bf16[64,96,128]{2,1,0:T(8,128)(2,1)} %all-to-all-done.2.parts_ref, bf16[512,128]{1,0:T(8,128)(2,1)S(1)} %get-tuple-element.21.hot_ref), custom_call_target="tpu_custom_call" | custom-call | tf_op jit(solution)/shard_map/pallas_call | solution.py:267
  (21 shorter events, 4.2 us)
Async XLA Ops:
  0.6 10.9 %copy-start = (bf16[128,3072]{1,0:T(8,128)(2,1)S(1)}, bf16[128,3072]{1,0:T(8,128)(2,1)}, u32[]{:S(2)}) copy-start(bf16[128,3072]{1,0:T(8,128)(2,1)} %param.5) | copy-start | bytes 2359300
  3.5 18.0 %all-to-all-start = ((bf16[8,64,384]{2,1,0:T(8,128)(2,1)}), bf16[8,64,384]{2,1,0:T(8,128)(2,1)S(1)}, u32[]{:S(2)}, u32[]{:S(2)}) async-start(bf16[8,64,384]{2,1,0:T(8,128)(2,1)} %bitcast.4), calls=%async_computation | async-start | bytes 786432 | tf_op jit(solution)/shard_map/all_to_all | solution.py:280
  12.2 1.1 %copy-start.5 = (bf16[512,1536]{1,0:T(8,128)(2,1)}, bf16[512,1536]{1,0:T(8,128)(2,1)S(1)}, u32[]{:S(2)}) copy-start(bf16[512,1536]{1,0:T(8,128)(2,1)S(1)} %get-tuple-element.14) | copy-start | bytes 4718596
  21.4 27.7 %all-to-all-start.1 = ((bf16[8,64,1536]{2,1,0:T(8,128)(2,1)}), bf16[8,64,1536]{2,1,0:T(8,128)(2,1)S(1)}, u32[]{:S(2)}, u32[]{:S(2)}) async-start(bf16[8,64,1536]{2,1,0:T(8,128)(2,1)} %bitcast.13), calls=%async_computation.1 | async-start | bytes 3145728 | tf_op jit(solution)/shard_map/all_to_all | solution.py:280
  25.0 18.5 %collective-permute-start.3 = (bf16[512,384]{1,0:T(8,128)(2,1)S(1)}, bf16[512,384]{1,0:T(8,128)(2,1)S(1)}, u32[]{:S(2)}, u32[]{:S(2)}) collective-permute-start(bf16[512,384]{1,0:T(8,128)(2,1)S(1)} %bitcast.14), channel_id=1, source_target_pairs={{0,48},{16,0},{32,16},{48,32},{1,49},{17,1},{33,17},{49,33},{2,50}... | collective-permute-start | bytes 1179656 | tf_op jit(solution)/shard_map/ppermute | solution.py:294
  27.9 15.7 %collective-permute-start.2 = (bf16[512,384]{1,0:T(8,128)(2,1)S(1)}, bf16[512,384]{1,0:T(8,128)(2,1)S(1)}, u32[]{:S(2)}, u32[]{:S(2)}) collective-permute-start(bf16[512,384]{1,0:T(8,128)(2,1)S(1)} %bitcast.15), channel_id=1, source_target_pairs={{0,32},{16,48},{32,0},{48,16},{1,33},{17,49},{33,1},{49,17},{2,34}... | collective-permute-start | bytes 1179656 | tf_op jit(solution)/shard_map/ppermute | solution.py:294
  28.7 18.6 %collective-permute-start.1 = (bf16[512,384]{1,0:T(8,128)(2,1)S(1)}, bf16[512,384]{1,0:T(8,128)(2,1)S(1)}, u32[]{:S(2)}, u32[]{:S(2)}) collective-permute-start(bf16[512,384]{1,0:T(8,128)(2,1)S(1)} %bitcast.16), channel_id=1, source_target_pairs={{0,16},{16,32},{32,48},{48,0},{1,17},{17,33},{33,49},{49,1},{2,18}... | collective-permute-start | bytes 1179656 | tf_op jit(solution)/shard_map/ppermute | solution.py:294
  49.1 5.8 %collective-permute-start.4 = (bf16[512,1536]{1,0:T(8,128)(2,1)}, bf16[512,1536]{1,0:T(8,128)(2,1)}, u32[]{:S(2)}, u32[]{:S(2)}) collective-permute-start(bf16[512,1536]{1,0:T(8,128)(2,1)} %shard_map.71.own_ref), channel_id=1, source_target_pairs={{0,8},{8,0},{1,9},{9,1},{2,10},{10,2},{3,11},{11,3},{4,12},{12,4},... | collective-permute-start | bytes 4718600 | tf_op jit(solution)/shard_map/ppermute | solution.py:298
  49.1 9.7 %collective-permute-start = (bf16[512,1536]{1,0:T(8,128)(2,1)S(1)}, bf16[512,1536]{1,0:T(8,128)(2,1)S(1)}, u32[]{:S(2)}, u32[]{:S(2)}) collective-permute-start(bf16[512,1536]{1,0:T(8,128)(2,1)S(1)} %bitcast.10), channel_id=1, source_target_pairs={{0,8},{8,0},{1,9},{9,1},{2,10},{10,2},{3,11},{11,3},{4,12},{12,4},... | collective-permute-start | bytes 4718600 | tf_op jit(solution)/shard_map/ppermute | solution.py:300
  49.6 2.8 %copy-start.1 = (bf16[1,2,3072,512]{3,2,1,0:T(8,128)(2,1)S(1)}, bf16[1,2,3072,512]{3,2,1,0:T(8,128)(2,1)}, u32[]{:S(2)}) copy-start(bf16[1,2,3072,512]{3,2,1,0:T(8,128)(2,1)} %panel_ref.7) | copy-start | bytes 18874372
  52.4 2.8 %copy-start.2 = (bf16[1,2,3072,512]{3,2,1,0:T(8,128)(2,1)S(1)}, bf16[1,2,3072,512]{3,2,1,0:T(8,128)(2,1)}, u32[]{:S(2)}) copy-start(bf16[1,2,3072,512]{3,2,1,0:T(8,128)(2,1)} %panel_ref.7) | copy-start | bytes 18874372
  58.9 2.7 %copy-start.3 = (bf16[512,1536]{1,0:T(8,128)(2,1)}, bf16[512,1536]{1,0:T(8,128)(2,1)S(1)}, u32[]{:S(2)}) copy-start(bf16[512,1536]{1,0:T(8,128)(2,1)S(1)} %collective-permute-done.oth_ref) | copy-start | bytes 4718596
  61.6 3.5 %collective-permute-start.5 = (bf16[8,8,96,128]{3,2,1,0:T(8,128)(2,1)S(1)}, bf16[8,8,96,128]{3,2,1,0:T(8,128)(2,1)S(1)}, u32[]{:S(2)}, u32[]{:S(2)}) collective-permute-start(bf16[8,8,96,128]{3,2,1,0:T(8,128)(2,1)S(1)} %get-tuple-element.17), channel_id=1, source_target_pairs={{0,8},{8,0},{1,9},{9,1},{2,10},{10,2},{3,11},{11,3},{4,12},{12,4},... | collective-permute-start | bytes 4718600 | tf_op jit(solution)/shard_map/ppermute | solution.py:303
  66.7 33.1 %all-to-all-start.2 = ((bf16[64,96,128]{2,1,0:T(8,128)(2,1)}), bf16[64,96,128]{2,1,0:T(8,128)(2,1)}, u32[]{:S(2)}, u32[]{:S(2)}) async-start(bf16[64,96,128]{2,1,0:T(8,128)(2,1)} %bitcast.18), calls=%async_computation.2 | async-start | bytes 3145728 | tf_op jit(solution)/shard_map/all_to_all | solution.py:280
  75.1 1.4 %copy-start.4 = (bf16[512,1536]{1,0:T(8,128)(2,1)S(1)}, bf16[512,1536]{1,0:T(8,128)(2,1)}, u32[]{:S(2)}) copy-start(bf16[512,1536]{1,0:T(8,128)(2,1)} %copy-done.3) | copy-start | bytes 4718596

commit v4 on v3

--- a/solution.py
+++ b/solution.py
@@ -1,3 +1,5 @@
+import itertools
+
 import jax
 import jax.numpy as jnp
 from jax import lax
@@ -20,7 +22,27 @@
 BLK = ("yhi", "z")
 AXES = ("ylo", "x", "core", "yhi", "z")
 SIZES = (2, 4, 2, 2, 4)
+
+SHIFTS = ((0, 0), (0, 1), (0, 3), (1, 2), (1, 1), (1, 3), (0, 2), (1, 0))
 MIB = 1024 * 1024
+
+
+def moves(flip, dz):
+    def flat(place):
+        number = 0
+        for part, size in zip(place, SIZES):
+            number = number * size + part
+        return number
+
+    return [
+        (flat((yl, x, c, yh, z)), flat((yl ^ flip, x, c, yh ^ flip, (z + dz) % 4)))
+        for yl, x, c, yh, z in itertools.product(*map(range, SIZES))
+    ]
+
+
+def block_rows(place_ref, flip, dz):
+    block = ((place_ref[2] + flip) % 2) * 4 + (place_ref[3] + dz) % 4
+    return pl.ds(pl.multiple_of(block * CAP, CAP), CAP)
 
 
 def matmul(a, b, ca, cb):
@@ -64,14 +86,26 @@
     return jnp.where(place == slot[e : e + 1, :], 1.0, 0.0).astype(F32)
 
 
-def dispatch_x(table, tokens):
-    def body(table_ref, tok_ref, out_ref, hot_ref):
+def dispatch_x(place, table, tokens):
+    def body(place_ref, table_ref, tok_ref, *rest):
+        outs, hot_ref = rest[:EXPERTS], rest[EXPERTS]
         _, slot = slot_rows(table_ref[...])
         for e in range(EXPERTS):
             hot_ref[e * CAP : (e + 1) * CAP, :] = hot_chunk(slot, e).astype(BF)
-        out_ref[...] = matmul(hot_ref[...], tok_ref[...], 1, 0).astype(BF)
-
-    return call(body, [VM, VM], [((ROWS, HALF), BF), ((ROWS, TOK), BF)], [])(table, tokens)
+        for out_ref, (flip, dz) in zip(outs, SHIFTS):
+            hot = hot_ref[block_rows(place_ref, flip, dz), :]
+            out_ref[...] = matmul(hot, tok_ref[...], 1, 0).astype(BF)
+
+    outs = [((CAP, HALF), BF)] * EXPERTS + [((ROWS, TOK), BF)]
+    return call(body, [SM, VM, VM], outs, [])(place, table, tokens)
+
+
+def gather_blocks(place, pieces):
+    def body(place_ref, *refs):
+        for ref, (flip, dz) in zip(refs, SHIFTS):
+            refs[EXPERTS][block_rows(place_ref, flip, -dz % 4), :] = ref[...]
+
+    return call(body, [SM] + [VM] * EXPERTS, [((ROWS, HALF), BF)], [])(place, *pieces)[0]
 
 
 def dispatch_d(table, out_grad):
@@ -102,13 +136,21 @@
     )(table, out_grad)[0]
 
 
-def assemble(place, pieces):
-    def body(place_ref, *refs):
-        for r in range(XS):
-            start = ((place_ref[1] + XS - r) % XS) * QUART
-            refs[XS][:, pl.ds(pl.multiple_of(start, LANES), QUART)] = refs[r][...]
-
-    return call(body, [SM] + [VM] * XS, [((ROWS, HALF), BF)], [])(place, *pieces)[0]
+def assemble(place, mine, left, right, far_top, far_low):
+    def body(place_ref, mine_ref, left_ref, right_ref, top_ref, low_ref, out_ref):
+        def columns(shift):
+            start = ((place_ref[1] + shift) % XS) * QUART
+            return pl.ds(pl.multiple_of(start, LANES), QUART)
+
+        out_ref[:, columns(0)] = mine_ref[...]
+        out_ref[:, columns(3)] = left_ref[...]
+        out_ref[:, columns(1)] = right_ref[...]
+        out_ref[: ROWS // 2, columns(2)] = top_ref[...]
+        out_ref[ROWS // 2 :, columns(2)] = low_ref[...]
+
+    return call(body, [SM] + [VM] * 5, [((ROWS, HALF), BF)], [])(
+        place, mine, left, right, far_top, far_low
+    )[0]
 
 
 def half_of(panel_ref, which, half):
@@ -253,15 +295,19 @@
         half = CAP // 2
 
         def summed(hots, rows):
-            return matmul(rows.reshape(-1, LANES), hots.reshape(-1, TOK), 0, 0)
-
-        hot = hot_ref[...].reshape(EXPERTS, 1, CAP, TOK)
-        hot = jnp.broadcast_to(hot, (EXPERTS, CHIPS, CAP, TOK))
+            hots, rows = hots.reshape(-1, TOK), rows.reshape(-1, LANES)
+            high = rows.astype(BF)
+            low = (rows - high.astype(F32)).astype(BF)
+            return matmul(high, hots, 0, 0) + matmul(low, hots, 0, 0)
+
         parts = parts_ref[...].reshape(EXPERTS, CHIPS, PACK, LANES)
-        packed = parts[:, :, CAP:, :]
-        out_ref[:LANES, :] = summed(hot, parts[:, :, :CAP, :]).astype(BF)
-        low = summed(hot[:, :, :half, :], packed)
-        high = summed(hot[:, :, half:, :], packed)
+        total = parts[:, 0].astype(F32)
+        for j in range(1, CHIPS):
+            total += parts[:, j].astype(F32)
+        hot = hot_ref[...].reshape(EXPERTS, CAP, TOK)
+        out_ref[:LANES, :] = summed(hot, total[:, :CAP, :]).astype(BF)
+        low = summed(hot[:, :half, :], total[:, CAP:, :])
+        high = summed(hot[:, half:, :], total[:, CAP:, :])
         out_ref[LANES:, :] = (low[:REST, :] + high[REST:, :]).astype(BF)
 
     return call(body, [VM, VM], [((SLICE, TOK), BF)], [])(parts, hot)[0].T
@@ -269,7 +315,8 @@
 
 def shards(tokens, expert_ids, gate_levels, out_grad, panels):
     core, x = lax.axis_index("core"), lax.axis_index("x")
-    place = jnp.stack([core, x]).astype(jnp.int32)
+    place = [core, x, lax.axis_index("yhi"), lax.axis_index("z")]
+    place = jnp.stack(place).astype(jnp.int32)
     table = jnp.concatenate([expert_ids.T, gate_levels.T], axis=0)
     swap = [(0, 1), (1, 0)]
 
@@ -283,18 +330,23 @@
     d_small = dispatch_d(table, grad).reshape(EXPERTS, CAP, QUART)
     d_first = exchange(d_small, BLK).reshape(ROWS, QUART)
     tok = lax.dynamic_slice(after(tokens, d_small), (0, core * HALF), (TOK, HALF))
-    x_rows, hot = dispatch_x(table, tok)
-    x_sent = after(x_rows, d_first).reshape(EXPERTS, CAP, HALF)
-    x_own = exchange(x_sent, BLK).reshape(ROWS, HALF)
-    d_first = after(d_first, x_rows)
-    d_own = assemble(
-        place,
-        [d_first]
-        + [
-            lax.ppermute(d_first, "x", [(i, (i + r) % XS) for i in range(XS)])
-            for r in range(1, XS)
-        ],
-    )
+    *x_msgs, hot = dispatch_x(place, table, tok)
+
+    def send_x(k, *deps):
+        piece = after(x_msgs[k], *deps) if deps else x_msgs[k]
+        return lax.ppermute(piece, AXES, moves(*SHIFTS[k]))
+
+    got = [x_msgs[0]] + [send_x(k) for k in (1, 2, 3)]
+    up_x = [(i, (i + 1) % XS) for i in range(XS)]
+    down_x = [(i, (i - 1) % XS) for i in range(XS)]
+    d_first = after(d_first, got[1])
+    left, right = lax.ppermute(d_first, "x", up_x), lax.ppermute(d_first, "x", down_x)
+    for k in (4, 5, 6, 7):
+        got.append(send_x(k, got[k - 3]))
+    far_top = lax.ppermute(right[: ROWS // 2], "x", down_x)
+    far_low = lax.ppermute(left[ROWS // 2 :], "x", up_x)
+    x_own = gather_blocks(place, got)
+    d_own = assemble(place, d_first, left, right, far_top, far_low)
     d_oth = lax.ppermute(d_own, "core", swap)
     back = back_full(place, d_own, d_oth, panels)
     x_oth = lax.ppermute(x_own, "core", swap)

time: 103 us -> 98.3 us (0.954)
  starting transfers between devices: 25.1 us -> 35.6 us
  waiting for transfers between devices: 38.1 us -> 30.6 us
  local copies, waits for them, and re-layouts: 6.57 us -> 2.42 us
  Pallas kernels: 29.5 us -> 26 us
    ppermute x3 -> x11, starting transfers between devices: 4.51 us -> 18.8 us  [the longest x7 12.2 us: send_x(): return lax.ppermute(piece, AXES, moves(*SHIFTS[k]))]
    all_to_all x3 -> x2, waiting for transfers between devices: 17.9 us -> 12 us  [exchange(): return lax.all_to_all(rows, axes, split_axis=0, concat_axis=0, tiled=True)]
    unnamed x12 -> x16, local copies, waits for them, and re-layouts: 5.64 us -> 1.44 us
    all_to_all x3 -> x2, starting transfers between devices: 20 us -> 16.1 us  [exchange(): return lax.all_to_all(rows, axes, split_axis=0, concat_axis=0, tiled=True)]
    pallas_call x2, Pallas kernels: 13.4 us -> 11.4 us  [weight_grads(): pl.pallas_call(body, grid_spec=pltpu.PrefetchScalarGridSpec(num_scalar_pr...]
    pallas_call x1, Pallas kernels: 3.68 us -> 2.33 us  [back_full(): call(body, [SM, VM, VM, VM], [((ROWS, HID), F32)], [], flops=2 * ROWS * D...]
    ppermute x3 -> x11, waiting for transfers between devices: 17.6 us -> 17.3 us  [the longest x7 12.6 us: send_x(): return lax.ppermute(piece, AXES, moves(*SHIFTS[k]))]
    pallas_call x2 -> x3, Pallas kernels: 2.52 us -> 2.6 us  [the longest x1 1.26 us: dispatch_x(): return call(body, [SM, VM, VM], outs, [])(place, table, tokens)]
  transfers between devices with their start and end apart: 9 -> 16, of which waited for: 6 -> 8; matrix products, arithmetic and copies ran while one was open for 0% -> 0% of each run, Pallas kernels for 22% -> 20%
where the time goes in v4:
time: 98.3 us; the launch traced here: 97.9 us
  starting transfers between devices  35.6 us (36%)
  waiting for transfers between devices  30.6 us (31%)
  Pallas kernels  26 us (26%)
  other arithmetic  2.43 us (2%)
  local copies, waits for them, and re-layouts  2.42 us (2%)
    all_to_all x2, starting transfers between devices, exchange(): return lax.all_to_all(rows, axes, split_axis=0, concat_axis=0, tiled=True)  16.1 us
    ppermute x7, waiting for transfers between devices, send_x(): return lax.ppermute(piece, AXES, moves(*SHIFTS[k]))  12.6 us
    ppermute x7, starting transfers between devices, send_x(): return lax.ppermute(piece, AXES, moves(*SHIFTS[k]))  12.2 us
    all_to_all x2, waiting for transfers between devices, exchange(): return lax.all_to_all(rows, axes, split_axis=0, concat_axis=0, tiled=True)  12 us
    pallas_call x2, Pallas kernels, weight_grads(): pl.pallas_call(body, grid_spec=pltpu.PrefetchScalarGridSpec(num_scalar_pr...  11.4 us
    ppermute x1, starting transfers between devices, shards(): far_top = lax.ppermute(right[:ROWS // 2], 'x', down_x)  3.76 us
    ppermute x1, waiting for transfers between devices, shards(): lax.ppermute(d_first, 'x', down_x)  3.46 us
    ppermute x1, starting transfers between devices, shards(): lax.ppermute(d_first, 'x', down_x)  2.76 us
  transfers between devices with their start and end apart: 16, of which 8 were waited for; matrix products, arithmetic and copies ran while one was open for 0% of the time, Pallas kernels for 20%

profile of v4, /device:TPU:0, one launch (start us, length us, event | category | flops | bytes accessed | tf_op | source)
XLA Modules:
  0.0 97.9 jit_solution(15420507823151616188)
XLA Ops:
  3.5 8.0 %all-to-all-start = ((bf16[8,64,384]{2,1,0:T(8,128)(2,1)}), bf16[8,64,384]{2,1,0:T(8,128)(2,1)S(1)}, u32[]{:S(2)}, u32[]{:S(2)}) async-start(bf16[8,64,384]{2,1,0:T(8,128)(2,1)} %bitcast.6), calls=%async_computation | async-start | bytes 786432 | tf_op jit(solution)/shard_map/all_to_all | solution.py:327
  11.6 1.3 %shard_map.69 = (bf16[64,1536]{1,0:T(8,128)(2,1)S(1)}, bf16[64,1536]{1,0:T(8,128)(2,1)S(1)}, bf16[64,1536]{1,0:T(8,128)(2,1)S(1)}, bf16[64,1536]{1,0:T(8,128)(2,...) custom-call(s32[4]{0:T(128)S(1)} %pad_add_fusion.1.place_ref, ...), custom_call_target="tpu_custom_call" | custom-call | tf_op jit(solution)/shard_map/pallas_call | solution.py:100
  12.9 2.1 %collective-permute-start = (bf16[64,1536]{1,0:T(8,128)(2,1)S(1)}, bf16[64,1536]{1,0:T(8,128)(2,1)S(1)}, u32[]{:S(2)}, u32[]{:S(2)}) collective-permute-start(bf16[64,1536]{1,0:T(8,128)(2,1)S(1)} %get-tuple-element.24), channel_id=1, source_target_pairs={{0,1},{1,2},{2,3},{3,0},{4,5},{5,6},{6,7},{7,4},{8,9},{9,10},{10,1... | collective-permute-start | bytes 589832 | tf_op jit(solution)/shard_map/ppermute | solution.py:337
  15.0 8.7 %collective-permute-done.refs_1_ = bf16[64,1536]{1,0:T(8,128)(2,1)S(1)} collective-permute-done((bf16[64,1536]{1,0:T(8,128)(2,1)S(1)}, bf16[64,1536]{1,0:T(8,128)(2,1)S(1)}, u32[]{:S(2)}, u32[]{:S(2)}) %collective-permute-start) | collective-permute-done | bytes 196640 | tf_op jit(solution)/shard_map/ppermute | solution.py:337
  23.7 2.8 %collective-permute-start.9 = (bf16[512,384]{1,0:T(8,128)(2,1)S(1)}, bf16[512,384]{1,0:T(8,128)(2,1)S(1)}, u32[]{:S(2)}, u32[]{:S(2)}) collective-permute-start(bf16[512,384]{1,0:T(8,128)(2,1)S(1)} %bitcast.10), channel_id=1, source_target_pairs={{0,48},{16,0},{32,16},{48,32},{1,49},{17,1},{33,17},{49,33},{2,50}... | collective-permute-start | bytes 1179656 | tf_op jit(solution)/shard_map/ppermute | solution.py:343
  27.5 2.4 %collective-permute-start.2 = (bf16[64,1536]{1,0:T(8,128)(2,1)S(1)}, bf16[64,1536]{1,0:T(8,128)(2,1)S(1)}, u32[]{:S(2)}, u32[]{:S(2)}) collective-permute-start(bf16[64,1536]{1,0:T(8,128)(2,1)S(1)} %get-tuple-element.26), channel_id=1, source_target_pairs={{0,70},{1,71},{2,68},{3,69},{4,66},{5,67},{6,64},{7,65},{8,78},{9,... | collective-permute-start | bytes 589832 | tf_op jit(solution)/shard_map/ppermute | solution.py:337
  31.0 3.5 %collective-permute-done.9.right_ref = bf16[512,384]{1,0:T(8,128)(2,1)S(1)} collective-permute-done((bf16[512,384]{1,0:T(8,128)(2,1)S(1)}, bf16[512,384]{1,0:T(8,128)(2,1)S(1)}, u32[]{:S(2)}, u32[]{:S(2)}) %collective-permute-start.9) | collective-permute-done | bytes 393248 | tf_op jit(solution)/shard_map/ppermute | solution.py:343
  34.5 3.8 %collective-permute-start.10 = (bf16[256,384]{1,0:T(8,128)(2,1)S(1)}, bf16[256,384]{1,0:T(8,128)(2,1)S(1)}, u32[]{:S(2)}, u32[]{:S(2)}) collective-permute-start(bf16[256,384]{1,0:T(8,128)(2,1)S(1)} %slice.8), channel_id=1, source_target_pairs={{0,48},{16,0},{32,16},{48,32},{1,49},{17,1},{33,17},{49,33},{2,50}... | collective-permute-start | bytes 589832 | tf_op jit(solution)/shard_map/ppermute | solution.py:346
  38.3 2.9 %collective-permute-start.4 = (bf16[64,1536]{1,0:T(8,128)(2,1)S(1)}, bf16[64,1536]{1,0:T(8,128)(2,1)S(1)}, u32[]{:S(2)}, u32[]{:S(2)}) collective-permute-start(bf16[64,1536]{1,0:T(8,128)(2,1)S(1)} %get-tuple-element.30), channel_id=1, source_target_pairs={{0,71},{1,68},{2,69},{3,70},{4,67},{5,64},{6,65},{7,66},{8,79},{9,... | collective-permute-start | bytes 589832 | tf_op jit(solution)/shard_map/ppermute | solution.py:337
  42.0 2.0 %collective-permute-start.6 = (bf16[64,1536]{1,0:T(8,128)(2,1)S(1)}, bf16[64,1536]{1,0:T(8,128)(2,1)S(1)}, u32[]{:S(2)}, u32[]{:S(2)}) collective-permute-start(bf16[64,1536]{1,0:T(8,128)(2,1)S(1)} %get-tuple-element.34), channel_id=1, source_target_pairs={{0,68},{1,69},{2,70},{3,71},{4,64},{5,65},{6,66},{7,67},{8,76},{9,... | collective-permute-start | bytes 589832 | tf_op jit(solution)/shard_map/ppermute | solution.py:337
  46.0 1.8 %collective-permute-done.4.refs_5_ = bf16[64,1536]{1,0:T(8,128)(2,1)S(1)} collective-permute-done((bf16[64,1536]{1,0:T(8,128)(2,1)S(1)}, bf16[64,1536]{1,0:T(8,128)(2,1)S(1)}, u32[]{:S(2)}, u32[]{:S(2)}) %collective-permute-start.4) | collective-permute-done | bytes 196640 | tf_op jit(solution)/shard_map/ppermute | solution.py:337
  48.5 1.4 %collective-permute-done.6.refs_7_ = bf16[64,1536]{1,0:T(8,128)(2,1)S(1)} collective-permute-done((bf16[64,1536]{1,0:T(8,128)(2,1)S(1)}, bf16[64,1536]{1,0:T(8,128)(2,1)S(1)}, u32[]{:S(2)}, u32[]{:S(2)}) %collective-permute-start.6) | collective-permute-done | bytes 196640 | tf_op jit(solution)/shard_map/ppermute | solution.py:337
  50.6 1.5 %shard_map.71.part_ref = f32[512,512]{1,0:T(8,128)S(1)} custom-call(s32[4]{0:T(128)S(1)} %pad_add_fusion.1.place_ref, bf16[512,1536]{1,0:T(8,128)(2,1)S(1)} %shard_map.70.own_ref, bf16[1,2,3072,512]{3,2,1,0:T(8,128)(2,1)S(1)} %copy-done.1), custom_call_target="tpu_custom_call" | custom-call | flops 805306368 | bytes 1572864 | tf_op jit(solution)/shard_map/pallas_call | solution.py:189
  52.2 2.3 %shard_map.73.back_ref = f32[512,512]{1,0:T(8,128)S(1)} custom-call(s32[4]{0:T(128)S(1)} %pad_add_fusion.1.place_ref, bf16[512,1536]{1,0:T(8,128)(2,1)S(1)} %shard_map.72.own_ref, bf16[512,1536]{1,0:T(8,128)(2,1)S(1)} %collective-permute-done.12.oth_ref, bf16[1,2,3072,512]{3,2,1,0:T(8,128)(2,1)S(1)} %copy-done.1), custom_call_target="tpu_custom_call" | custom-call | flops 1610612736 | bytes 3145728 | tf_op jit(solution)/shard_map/pallas_call | solution.py:175
  54.5 2.7 %shard_map.74 = (bf16[512,512]{1,0:T(8,128)(2,1)S(1)}, bf16[512,512]{1,0:T(8,128)(2,1)S(1)}, bf16[8,8,96,128]{3,2,1,0:T(8,128)(2,1)S(1)}) custom-call(s32[4]{0:T(128)S(1)} %pad_add_fusion.1.place_ref, f32[512,512]{1,0:T(8,128)S(1)} %shard_map.71.part_ref, bf16[512,1536]{1,0:T(8,128)(2,1)S(1)} %collective-permute-done.7.oth_ref, ...), custom_call_target="tpu_custom_call" | custom-call | flops 1610612736 | bytes 3145728 | tf_op jit(solution)/shard_map/pallas_call | solution.py:225
  57.8 1.8 %shard_map.75 = f32[8,8,96,128]{3,2,1,0:T(8,128)S(1)} custom-call(s32[4]{0:T(128)S(1)} %pad_add_fusion.1.place_ref, bf16[512,512]{1,0:T(8,128)(2,1)S(1)} %get-tuple-element.39.dpre_ref.right_ref, bf16[1,2,3072,512]{3,2,1,0:T(8,128)(2,1)S(1)} %copy-done.1), custom_call_target="tpu_custom_call" | custom-call | flops 805306368 | bytes 1572864 | tf_op jit(solution)/shard_map/pallas_call | solution.py:240
  59.6 1.3 %collective-permute-done.13 = bf16[8,8,96,128]{3,2,1,0:T(8,128)(2,1)S(1)} collective-permute-done((bf16[8,8,96,128]{3,2,1,0:T(8,128)(2,1)S(1)}, bf16[8,8,96,128]{3,2,1,0:T(8,128)(2,1)S(1)}, u32[]{:S(2)}, u32[]{:S(2)}) %collective-permute-start.13) | collective-permute-done | bytes 1572896 | tf_op jit(solution)/shard_map/ppermute | solution.py:355
  60.9 1.6 %add_convert_fusion = bf16[8,8,96,128]{3,2,1,0:T(8,128)(2,1)} fusion(f32[8,8,96,128]{3,2,1,0:T(8,128)S(1)} %shard_map.75, bf16[8,8,96,128]{3,2,1,0:T(8,128)(2,1)S(1)} %collective-permute-done.13), kind=kLoop, calls=%fused_computation | loop fusion | flops 2359296 | bytes 6291456 | tf_op jit(solution)/shard_map/convert_element_type | solution.py:356
  62.5 8.1 %all-to-all-start.1 = ((bf16[64,96,128]{2,1,0:T(8,128)(2,1)}), bf16[64,96,128]{2,1,0:T(8,128)(2,1)}, u32[]{:S(2)}, u32[]{:S(2)}) async-start(bf16[64,96,128]{2,1,0:T(8,128)(2,1)} %bitcast.13), calls=%async_computation.1 | async-start | bytes 3145728 | tf_op jit(solution)/shard_map/all_to_all | solution.py:327
  70.6 1.4 %copy-done.5 = bf16[512,1536]{1,0:T(8,128)(2,1)S(1)} copy-done((bf16[512,1536]{1,0:T(8,128)(2,1)S(1)}, bf16[512,1536]{1,0:T(8,128)(2,1)}, u32[]{:S(2)}) %copy-start.5) | copy-done | bytes 1572888
  72.0 5.7 %shard_map.76.rest_0_ = f32[1,2,3072,512]{3,2,1,0:T(8,128)} custom-call(s32[4]{0:T(128)S(1)} %pad_add_fusion.1.place_ref, bf16[512,1536]{1,0:T(8,128)(2,1)S(1)} %shard_map.70.own_ref, bf16[512,1536]{1,0:T(8,128)(2,1)S(1)} %copy-done.5, bf16[512,512]{1,0:T(8,128)(2,1)S(1)} %get-tuple-element.39.dpre_ref.right_ref), custom_call_target="tpu_custom_call" | custom-call | flops 1610612736 | bytes 6291456 | tf_op jit(solution)/shard_map/pallas_call | solution.py:271
  77.7 5.7 %shard_map.77 = f32[1,2,3072,512]{3,2,1,0:T(8,128)} custom-call(s32[4]{0:T(128)S(1)} %pad_add_fusion.1.place_ref, bf16[512,1536]{1,0:T(8,128)(2,1)S(1)} %copy-done.3, bf16[512,1536]{1,0:T(8,128)(2,1)S(1)} %copy-done.7, bf16[512,512]{1,0:T(8,128)(2,1)S(1)} %get-tuple-element.38.right_ref, ...), custom_call_target="tpu_custom_call", output_to_operand_aliasing={{}: (4, {})} | custom-call | flops 1610612736 | bytes 6291456 | tf_op jit(solution)/shard_map/pallas_call | solution.py:271
  83.4 12.0 %all-to-all-done.1.parts_ref = bf16[64,96,128]{2,1,0:T(8,128)(2,1)} async-done(((bf16[64,96,128]{2,1,0:T(8,128)(2,1)}), bf16[64,96,128]{2,1,0:T(8,128)(2,1)}, u32[]{:S(2)}, u32[]{:S(2)}) %all-to-all-start.1) | async-done | bytes 1572896 | tf_op jit(solution)/shard_map/all_to_all | solution.py:327
  95.4 2.5 %shard_map.78 = bf16[192,128]{1,0:T(8,128)(2,1)} custom-call(bf16[64,96,128]{2,1,0:T(8,128)(2,1)} %all-to-all-done.1.parts_ref, bf16[512,128]{1,0:T(8,128)(2,1)S(1)} %get-tuple-element.41.hot_ref), custom_call_target="tpu_custom_call" | custom-call | tf_op jit(solution)/shard_map/pallas_call | solution.py:313
  (42 shorter events, 9.9 us)
Async XLA Ops:
  0.6 10.9 %copy-start = (bf16[128,3072]{1,0:T(8,128)(2,1)S(1)}, bf16[128,3072]{1,0:T(8,128)(2,1)}, u32[]{:S(2)}) copy-start(bf16[128,3072]{1,0:T(8,128)(2,1)} %param.5) | copy-start | bytes 2359300
  3.5 20.2 %all-to-all-start = ((bf16[8,64,384]{2,1,0:T(8,128)(2,1)}), bf16[8,64,384]{2,1,0:T(8,128)(2,1)S(1)}, u32[]{:S(2)}, u32[]{:S(2)}) async-start(bf16[8,64,384]{2,1,0:T(8,128)(2,1)} %bitcast.6), calls=%async_computation | async-start | bytes 786432 | tf_op jit(solution)/shard_map/all_to_all | solution.py:327
  12.9 10.8 %collective-permute-start = (bf16[64,1536]{1,0:T(8,128)(2,1)S(1)}, bf16[64,1536]{1,0:T(8,128)(2,1)S(1)}, u32[]{:S(2)}, u32[]{:S(2)}) collective-permute-start(bf16[64,1536]{1,0:T(8,128)(2,1)S(1)} %get-tuple-element.24), channel_id=1, source_target_pairs={{0,1},{1,2},{2,3},{3,0},{4,5},{5,6},{6,7},{7,4},{8,9},{9,10},{10,1... | collective-permute-start | bytes 589832 | tf_op jit(solution)/shard_map/ppermute | solution.py:337
  23.7 10.7 %collective-permute-start.9 = (bf16[512,384]{1,0:T(8,128)(2,1)S(1)}, bf16[512,384]{1,0:T(8,128)(2,1)S(1)}, u32[]{:S(2)}, u32[]{:S(2)}) collective-permute-start(bf16[512,384]{1,0:T(8,128)(2,1)S(1)} %bitcast.10), channel_id=1, source_target_pairs={{0,48},{16,0},{32,16},{48,32},{1,49},{17,1},{33,17},{49,33},{2,50}... | collective-permute-start | bytes 1179656 | tf_op jit(solution)/shard_map/ppermute | solution.py:343
  26.5 11.8 %collective-permute-start.8 = (bf16[512,384]{1,0:T(8,128)(2,1)S(1)}, bf16[512,384]{1,0:T(8,128)(2,1)S(1)}, u32[]{:S(2)}, u32[]{:S(2)}) collective-permute-start(bf16[512,384]{1,0:T(8,128)(2,1)S(1)} %bitcast.11), channel_id=1, source_target_pairs={{0,16},{16,32},{32,48},{48,0},{1,17},{17,33},{33,49},{49,1},{2,18}... | collective-permute-start | bytes 1179656 | tf_op jit(solution)/shard_map/ppermute | solution.py:343
  26.5 11.9 %collective-permute-start.1 = (bf16[64,1536]{1,0:T(8,128)(2,1)S(1)}, bf16[64,1536]{1,0:T(8,128)(2,1)S(1)}, u32[]{:S(2)}, u32[]{:S(2)}) collective-permute-start(bf16[64,1536]{1,0:T(8,128)(2,1)S(1)} %get-tuple-element.25), channel_id=1, source_target_pairs={{0,3},{1,0},{2,1},{3,2},{4,7},{5,4},{6,5},{7,6},{8,11},{9,8},{10,9... | collective-permute-start | bytes 589832 | tf_op jit(solution)/shard_map/ppermute | solution.py:337
  27.5 13.8 %collective-permute-start.2 = (bf16[64,1536]{1,0:T(8,128)(2,1)S(1)}, bf16[64,1536]{1,0:T(8,128)(2,1)S(1)}, u32[]{:S(2)}, u32[]{:S(2)}) collective-permute-start(bf16[64,1536]{1,0:T(8,128)(2,1)S(1)} %get-tuple-element.26), channel_id=1, source_target_pairs={{0,70},{1,71},{2,68},{3,69},{4,66},{5,67},{6,64},{7,65},{8,78},{9,... | collective-permute-start | bytes 589832 | tf_op jit(solution)/shard_map/ppermute | solution.py:337
  29.9 12.1 %collective-permute-start.3 = (bf16[64,1536]{1,0:T(8,128)(2,1)S(1)}, bf16[64,1536]{1,0:T(8,128)(2,1)S(1)}, u32[]{:S(2)}, u32[]{:S(2)}) collective-permute-start(bf16[64,1536]{1,0:T(8,128)(2,1)S(1)} %get-tuple-element.28), channel_id=1, source_target_pairs={{0,69},{1,70},{2,71},{3,68},{4,65},{5,66},{6,67},{7,64},{8,77},{9,... | collective-permute-start | bytes 589832 | tf_op jit(solution)/shard_map/ppermute | solution.py:337
  34.5 9.5 %collective-permute-start.10 = (bf16[256,384]{1,0:T(8,128)(2,1)S(1)}, bf16[256,384]{1,0:T(8,128)(2,1)S(1)}, u32[]{:S(2)}, u32[]{:S(2)}) collective-permute-start(bf16[256,384]{1,0:T(8,128)(2,1)S(1)} %slice.8), channel_id=1, source_target_pairs={{0,48},{16,0},{32,16},{48,32},{1,49},{17,1},{33,17},{49,33},{2,50}... | collective-permute-start | bytes 589832 | tf_op jit(solution)/shard_map/ppermute | solution.py:346
  38.2 6.9 %collective-permute-start.11 = (bf16[256,384]{1,0:T(8,128)(2,1)S(1)}, bf16[256,384]{1,0:T(8,128)(2,1)S(1)}, u32[]{:S(2)}, u32[]{:S(2)}) collective-permute-start(bf16[256,384]{1,0:T(8,128)(2,1)S(1)} %slice.9), channel_id=1, source_target_pairs={{0,16},{16,32},{32,48},{48,0},{1,17},{17,33},{33,49},{49,1},{2,18}... | collective-permute-start | bytes 589832 | tf_op jit(solution)/shard_map/ppermute | solution.py:347
  38.3 9.4 %collective-permute-start.4 = (bf16[64,1536]{1,0:T(8,128)(2,1)S(1)}, bf16[64,1536]{1,0:T(8,128)(2,1)S(1)}, u32[]{:S(2)}, u32[]{:S(2)}) collective-permute-start(bf16[64,1536]{1,0:T(8,128)(2,1)S(1)} %get-tuple-element.30), channel_id=1, source_target_pairs={{0,71},{1,68},{2,69},{3,70},{4,67},{5,64},{6,65},{7,66},{8,79},{9,... | collective-permute-start | bytes 589832 | tf_op jit(solution)/shard_map/ppermute | solution.py:337
  41.3 7.2 %collective-permute-start.5 = (bf16[64,1536]{1,0:T(8,128)(2,1)S(1)}, bf16[64,1536]{1,0:T(8,128)(2,1)S(1)}, u32[]{:S(2)}, u32[]{:S(2)}) collective-permute-start(bf16[64,1536]{1,0:T(8,128)(2,1)S(1)} %get-tuple-element.32), channel_id=1, source_target_pairs={{0,2},{1,3},{2,0},{3,1},{4,6},{5,7},{6,4},{7,5},{8,10},{9,11},{10,... | collective-permute-start | bytes 589832 | tf_op jit(solution)/shard_map/ppermute | solution.py:337
  42.0 7.9 %collective-permute-start.6 = (bf16[64,1536]{1,0:T(8,128)(2,1)S(1)}, bf16[64,1536]{1,0:T(8,128)(2,1)S(1)}, u32[]{:S(2)}, u32[]{:S(2)}) collective-permute-start(bf16[64,1536]{1,0:T(8,128)(2,1)S(1)} %get-tuple-element.34), channel_id=1, source_target_pairs={{0,68},{1,69},{2,70},{3,71},{4,64},{5,65},{6,66},{7,67},{8,76},{9,... | collective-permute-start | bytes 589832 | tf_op jit(solution)/shard_map/ppermute | solution.py:337
  45.2 5.4 %copy-start.1 = (bf16[1,2,3072,512]{3,2,1,0:T(8,128)(2,1)S(1)}, bf16[1,2,3072,512]{3,2,1,0:T(8,128)(2,1)}, u32[]{:S(2)}) copy-start(bf16[1,2,3072,512]{3,2,1,0:T(8,128)(2,1)} %panel_ref.7) | copy-start | bytes 18874372
  45.9 6.3 %copy-start.2 = (bf16[512,1536]{1,0:T(8,128)(2,1)}, bf16[512,1536]{1,0:T(8,128)(2,1)S(1)}, u32[]{:S(2)}) copy-start(bf16[512,1536]{1,0:T(8,128)(2,1)S(1)} %shard_map.72.own_ref) | copy-start | bytes 4718596
  45.9 6.3 %collective-permute-start.12 = (bf16[512,1536]{1,0:T(8,128)(2,1)S(1)}, bf16[512,1536]{1,0:T(8,128)(2,1)S(1)}, u32[]{:S(2)}, u32[]{:S(2)}) collective-permute-start(bf16[512,1536]{1,0:T(8,128)(2,1)S(1)} %shard_map.72.own_ref), channel_id=1, source_target_pairs={{0,8},{8,0},{1,9},{9,1},{2,10},{10,2},{3,11},{11,3},{4,12},{12,4},... | collective-permute-start | bytes 4718600 | tf_op jit(solution)/shard_map/ppermute | solution.py:350
  50.5 4.0 %collective-permute-start.7 = (bf16[512,1536]{1,0:T(8,128)(2,1)S(1)}, bf16[512,1536]{1,0:T(8,128)(2,1)S(1)}, u32[]{:S(2)}, u32[]{:S(2)}) collective-permute-start(bf16[512,1536]{1,0:T(8,128)(2,1)S(1)} %shard_map.70.own_ref), channel_id=1, source_target_pairs={{0,8},{8,0},{1,9},{9,1},{2,10},{10,2},{3,11},{11,3},{4,12},{12,4},... | collective-permute-start | bytes 4718600 | tf_op jit(solution)/shard_map/ppermute | solution.py:352
  52.2 2.3 %copy-start.6 = (bf16[512,1536]{1,0:T(8,128)(2,1)}, bf16[512,1536]{1,0:T(8,128)(2,1)S(1)}, u32[]{:S(2)}) copy-start(bf16[512,1536]{1,0:T(8,128)(2,1)S(1)} %collective-permute-done.12.oth_ref) | copy-start | bytes 4718596
  54.5 2.7 %copy-start.4 = (bf16[512,1536]{1,0:T(8,128)(2,1)}, bf16[512,1536]{1,0:T(8,128)(2,1)S(1)}, u32[]{:S(2)}) copy-start(bf16[512,1536]{1,0:T(8,128)(2,1)S(1)} %collective-permute-done.7.oth_ref) | copy-start | bytes 4718596
  57.3 3.6 %collective-permute-start.13 = (bf16[8,8,96,128]{3,2,1,0:T(8,128)(2,1)S(1)}, bf16[8,8,96,128]{3,2,1,0:T(8,128)(2,1)S(1)}, u32[]{:S(2)}, u32[]{:S(2)}) collective-permute-start(bf16[8,8,96,128]{3,2,1,0:T(8,128)(2,1)S(1)} %get-tuple-element.37), channel_id=1, source_target_pairs={{0,8},{8,0},{1,9},{9,1},{2,10},{10,2},{3,11},{11,3},{4,12},{12,4},... | collective-permute-start | bytes 4718600 | tf_op jit(solution)/shard_map/ppermute | solution.py:355
  62.5 32.9 %all-to-all-start.1 = ((bf16[64,96,128]{2,1,0:T(8,128)(2,1)}), bf16[64,96,128]{2,1,0:T(8,128)(2,1)}, u32[]{:S(2)}, u32[]{:S(2)}) async-start(bf16[64,96,128]{2,1,0:T(8,128)(2,1)} %bitcast.13), calls=%async_computation.1 | async-start | bytes 3145728 | tf_op jit(solution)/shard_map/all_to_all | solution.py:327
  70.6 1.4 %copy-start.5 = (bf16[512,1536]{1,0:T(8,128)(2,1)S(1)}, bf16[512,1536]{1,0:T(8,128)(2,1)}, u32[]{:S(2)}) copy-start(bf16[512,1536]{1,0:T(8,128)(2,1)} %copy-done.4) | copy-start | bytes 4718596
  72.0 5.7 %copy-start.3 = (bf16[512,1536]{1,0:T(8,128)(2,1)S(1)}, bf16[512,1536]{1,0:T(8,128)(2,1)}, u32[]{:S(2)}) copy-start(bf16[512,1536]{1,0:T(8,128)(2,1)} %copy-done.2) | copy-start | bytes 4718596
  72.0 5.7 %copy-start.7 = (bf16[512,1536]{1,0:T(8,128)(2,1)S(1)}, bf16[512,1536]{1,0:T(8,128)(2,1)}, u32[]{:S(2)}) copy-start(bf16[512,1536]{1,0:T(8,128)(2,1)} %copy-done.6) | copy-start | bytes 4718596

commit v5 on v4

--- a/solution.py
+++ b/solution.py
@@ -240,7 +240,7 @@
     return call(
         body,
         [SM, VM, VM],
-        [((EXPERTS, CHIPS, PACK, LANES), F32)],
+        [((EXPERTS, CHIPS, PACK, LANES), BF)],
         [pltpu.VMEM((HALF, HID), BF)],
         flops=ROWS * D * HID,
         nbytes=D * HID,
@@ -353,7 +353,7 @@
     part = up_own(place, x_own, panels)
     hidden, d_pre, dx_send = middle(place, part, x_oth, back, panels)
     dx_recv = lax.ppermute(dx_send, "core", swap)
-    chip_dx = (dx_mine(place, d_pre, panels) + dx_recv.astype(F32)).astype(BF)
+    chip_dx = (dx_mine(place, d_pre, panels).astype(F32) + dx_recv.astype(F32)).astype(BF)
     parts = exchange(chip_dx.reshape(DESTS, PACK, LANES), ("yhi", "z", "ylo", "x"))
     panel_grads = weight_grads(place, x_own, x_oth, after(d_pre, chip_dx), 0)
     panel_grads = weight_grads(place, d_own, d_oth, hidden, 1, panel_grads)

time: 98.3 us -> 98.3 us (level)
  no operation moved by 1% of the time
where the time goes in v5:
time: 98.3 us; the launch traced here: 97.9 us
  starting transfers between devices  35.6 us (36%)
  waiting for transfers between devices  30.7 us (31%)
  Pallas kernels  25.8 us (26%)
  other arithmetic  2.43 us (2%)
  local copies, waits for them, and re-layouts  2.42 us (2%)
    all_to_all x2, starting transfers between devices, exchange(): return lax.all_to_all(rows, axes, split_axis=0, concat_axis=0, tiled=True)  16.1 us
    ppermute x7, waiting for transfers between devices, send_x(): return lax.ppermute(piece, AXES, moves(*SHIFTS[k]))  12.6 us
    ppermute x7, starting transfers between devices, send_x(): return lax.ppermute(piece, AXES, moves(*SHIFTS[k]))  12.2 us
    all_to_all x2, waiting for transfers between devices, exchange(): return lax.all_to_all(rows, axes, split_axis=0, concat_axis=0, tiled=True)  12 us
    pallas_call x2, Pallas kernels, weight_grads(): pl.pallas_call(body, grid_spec=pltpu.PrefetchScalarGridSpec(num_scalar_pr...  11.4 us
    ppermute x1, starting transfers between devices, shards(): far_top = lax.ppermute(right[:ROWS // 2], 'x', down_x)  3.76 us
    ppermute x1, waiting for transfers between devices, shards(): lax.ppermute(d_first, 'x', down_x)  3.46 us
    ppermute x1, starting transfers between devices, shards(): lax.ppermute(d_first, 'x', down_x)  2.76 us
  transfers between devices with their start and end apart: 16, of which 8 were waited for; matrix products, arithmetic and copies ran while one was open for 0% of the time, Pallas kernels for 20%

profile of v5, /device:TPU:0, one launch (start us, length us, event | category | flops | bytes accessed | tf_op | source)
XLA Modules:
  0.0 97.9 jit_solution(7620227368255497926)
XLA Ops:
  3.5 8.0 %all-to-all-start = ((bf16[8,64,384]{2,1,0:T(8,128)(2,1)}), bf16[8,64,384]{2,1,0:T(8,128)(2,1)S(1)}, u32[]{:S(2)}, u32[]{:S(2)}) async-start(bf16[8,64,384]{2,1,0:T(8,128)(2,1)} %bitcast.6), calls=%async_computation | async-start | bytes 786432 | tf_op jit(solution)/shard_map/all_to_all | solution.py:327
  11.6 1.3 %shard_map.69 = (bf16[64,1536]{1,0:T(8,128)(2,1)S(1)}, bf16[64,1536]{1,0:T(8,128)(2,1)S(1)}, bf16[64,1536]{1,0:T(8,128)(2,1)S(1)}, bf16[64,1536]{1,0:T(8,128)(2,...) custom-call(s32[4]{0:T(128)S(1)} %pad_add_fusion.1.place_ref, ...), custom_call_target="tpu_custom_call" | custom-call | tf_op jit(solution)/shard_map/pallas_call | solution.py:100
  12.9 2.1 %collective-permute-start = (bf16[64,1536]{1,0:T(8,128)(2,1)S(1)}, bf16[64,1536]{1,0:T(8,128)(2,1)S(1)}, u32[]{:S(2)}, u32[]{:S(2)}) collective-permute-start(bf16[64,1536]{1,0:T(8,128)(2,1)S(1)} %get-tuple-element.24), channel_id=1, source_target_pairs={{0,1},{1,2},{2,3},{3,0},{4,5},{5,6},{6,7},{7,4},{8,9},{9,10},{10,1... | collective-permute-start | bytes 589832 | tf_op jit(solution)/shard_map/ppermute | solution.py:337
  15.0 8.7 %collective-permute-done.refs_1_ = bf16[64,1536]{1,0:T(8,128)(2,1)S(1)} collective-permute-done((bf16[64,1536]{1,0:T(8,128)(2,1)S(1)}, bf16[64,1536]{1,0:T(8,128)(2,1)S(1)}, u32[]{:S(2)}, u32[]{:S(2)}) %collective-permute-start) | collective-permute-done | bytes 196640 | tf_op jit(solution)/shard_map/ppermute | solution.py:337
  23.7 2.8 %collective-permute-start.9 = (bf16[512,384]{1,0:T(8,128)(2,1)S(1)}, bf16[512,384]{1,0:T(8,128)(2,1)S(1)}, u32[]{:S(2)}, u32[]{:S(2)}) collective-permute-start(bf16[512,384]{1,0:T(8,128)(2,1)S(1)} %bitcast.10), channel_id=1, source_target_pairs={{0,48},{16,0},{32,16},{48,32},{1,49},{17,1},{33,17},{49,33},{2,50}... | collective-permute-start | bytes 1179656 | tf_op jit(solution)/shard_map/ppermute | solution.py:343
  27.5 2.4 %collective-permute-start.2 = (bf16[64,1536]{1,0:T(8,128)(2,1)S(1)}, bf16[64,1536]{1,0:T(8,128)(2,1)S(1)}, u32[]{:S(2)}, u32[]{:S(2)}) collective-permute-start(bf16[64,1536]{1,0:T(8,128)(2,1)S(1)} %get-tuple-element.26), channel_id=1, source_target_pairs={{0,70},{1,71},{2,68},{3,69},{4,66},{5,67},{6,64},{7,65},{8,78},{9,... | collective-permute-start | bytes 589832 | tf_op jit(solution)/shard_map/ppermute | solution.py:337
  31.0 3.5 %collective-permute-done.9.right_ref = bf16[512,384]{1,0:T(8,128)(2,1)S(1)} collective-permute-done((bf16[512,384]{1,0:T(8,128)(2,1)S(1)}, bf16[512,384]{1,0:T(8,128)(2,1)S(1)}, u32[]{:S(2)}, u32[]{:S(2)}) %collective-permute-start.9) | collective-permute-done | bytes 393248 | tf_op jit(solution)/shard_map/ppermute | solution.py:343
  34.5 3.8 %collective-permute-start.10 = (bf16[256,384]{1,0:T(8,128)(2,1)S(1)}, bf16[256,384]{1,0:T(8,128)(2,1)S(1)}, u32[]{:S(2)}, u32[]{:S(2)}) collective-permute-start(bf16[256,384]{1,0:T(8,128)(2,1)S(1)} %slice.8), channel_id=1, source_target_pairs={{0,48},{16,0},{32,16},{48,32},{1,49},{17,1},{33,17},{49,33},{2,50}... | collective-permute-start | bytes 589832 | tf_op jit(solution)/shard_map/ppermute | solution.py:346
  38.3 2.9 %collective-permute-start.4 = (bf16[64,1536]{1,0:T(8,128)(2,1)S(1)}, bf16[64,1536]{1,0:T(8,128)(2,1)S(1)}, u32[]{:S(2)}, u32[]{:S(2)}) collective-permute-start(bf16[64,1536]{1,0:T(8,128)(2,1)S(1)} %get-tuple-element.30), channel_id=1, source_target_pairs={{0,71},{1,68},{2,69},{3,70},{4,67},{5,64},{6,65},{7,66},{8,79},{9,... | collective-permute-start | bytes 589832 | tf_op jit(solution)/shard_map/ppermute | solution.py:337
  42.0 2.0 %collective-permute-start.6 = (bf16[64,1536]{1,0:T(8,128)(2,1)S(1)}, bf16[64,1536]{1,0:T(8,128)(2,1)S(1)}, u32[]{:S(2)}, u32[]{:S(2)}) collective-permute-start(bf16[64,1536]{1,0:T(8,128)(2,1)S(1)} %get-tuple-element.34), channel_id=1, source_target_pairs={{0,68},{1,69},{2,70},{3,71},{4,64},{5,65},{6,66},{7,67},{8,76},{9,... | collective-permute-start | bytes 589832 | tf_op jit(solution)/shard_map/ppermute | solution.py:337
  46.0 1.8 %collective-permute-done.4.refs_5_ = bf16[64,1536]{1,0:T(8,128)(2,1)S(1)} collective-permute-done((bf16[64,1536]{1,0:T(8,128)(2,1)S(1)}, bf16[64,1536]{1,0:T(8,128)(2,1)S(1)}, u32[]{:S(2)}, u32[]{:S(2)}) %collective-permute-start.4) | collective-permute-done | bytes 196640 | tf_op jit(solution)/shard_map/ppermute | solution.py:337
  48.5 1.4 %collective-permute-done.6.refs_7_ = bf16[64,1536]{1,0:T(8,128)(2,1)S(1)} collective-permute-done((bf16[64,1536]{1,0:T(8,128)(2,1)S(1)}, bf16[64,1536]{1,0:T(8,128)(2,1)S(1)}, u32[]{:S(2)}, u32[]{:S(2)}) %collective-permute-start.6) | collective-permute-done | bytes 196640 | tf_op jit(solution)/shard_map/ppermute | solution.py:337
  50.6 1.5 %shard_map.71.part_ref = f32[512,512]{1,0:T(8,128)S(1)} custom-call(s32[4]{0:T(128)S(1)} %pad_add_fusion.1.place_ref, bf16[512,1536]{1,0:T(8,128)(2,1)S(1)} %shard_map.70.own_ref, bf16[1,2,3072,512]{3,2,1,0:T(8,128)(2,1)S(1)} %copy-done.1), custom_call_target="tpu_custom_call" | custom-call | flops 805306368 | bytes 1572864 | tf_op jit(solution)/shard_map/pallas_call | solution.py:189
  52.2 2.3 %shard_map.73.back_ref = f32[512,512]{1,0:T(8,128)S(1)} custom-call(s32[4]{0:T(128)S(1)} %pad_add_fusion.1.place_ref, bf16[512,1536]{1,0:T(8,128)(2,1)S(1)} %shard_map.72.own_ref, bf16[512,1536]{1,0:T(8,128)(2,1)S(1)} %collective-permute-done.12.oth_ref, bf16[1,2,3072,512]{3,2,1,0:T(8,128)(2,1)S(1)} %copy-done.1), custom_call_target="tpu_custom_call" | custom-call | flops 1610612736 | bytes 3145728 | tf_op jit(solution)/shard_map/pallas_call | solution.py:175
  54.5 2.7 %shard_map.74 = (bf16[512,512]{1,0:T(8,128)(2,1)S(1)}, bf16[512,512]{1,0:T(8,128)(2,1)S(1)}, bf16[8,8,96,128]{3,2,1,0:T(8,128)(2,1)S(1)}) custom-call(s32[4]{0:T(128)S(1)} %pad_add_fusion.1.place_ref, f32[512,512]{1,0:T(8,128)S(1)} %shard_map.71.part_ref, bf16[512,1536]{1,0:T(8,128)(2,1)S(1)} %collective-permute-done.7.oth_ref, ...), custom_call_target="tpu_custom_call" | custom-call | flops 1610612736 | bytes 3145728 | tf_op jit(solution)/shard_map/pallas_call | solution.py:225
  57.8 1.6 %shard_map.75 = bf16[8,8,96,128]{3,2,1,0:T(8,128)(2,1)S(1)} custom-call(s32[4]{0:T(128)S(1)} %pad_add_fusion.1.place_ref, bf16[512,512]{1,0:T(8,128)(2,1)S(1)} %get-tuple-element.39.dpre_ref.right_ref, bf16[1,2,3072,512]{3,2,1,0:T(8,128)(2,1)S(1)} %copy-done.1), custom_call_target="tpu_custom_call" | custom-call | flops 805306368 | bytes 1572864 | tf_op jit(solution)/shard_map/pallas_call | solution.py:240
  59.5 1.4 %collective-permute-done.13 = bf16[8,8,96,128]{3,2,1,0:T(8,128)(2,1)S(1)} collective-permute-done((bf16[8,8,96,128]{3,2,1,0:T(8,128)(2,1)S(1)}, bf16[8,8,96,128]{3,2,1,0:T(8,128)(2,1)S(1)}, u32[]{:S(2)}, u32[]{:S(2)}) %collective-permute-start.13) | collective-permute-done | bytes 1572896 | tf_op jit(solution)/shard_map/ppermute | solution.py:355
  60.9 1.6 %add_convert_fusion = bf16[8,8,96,128]{3,2,1,0:T(8,128)(2,1)} fusion(bf16[8,8,96,128]{3,2,1,0:T(8,128)(2,1)S(1)} %collective-permute-done.13, bf16[8,8,96,128]{3,2,1,0:T(8,128)(2,1)S(1)} %shard_map.75), kind=kLoop, calls=%fused_computation | loop fusion | flops 3145728 | bytes 4718592 | tf_op jit(solution)/shard_map/convert_element_type | solution.py:356
  62.5 8.1 %all-to-all-start.1 = ((bf16[64,96,128]{2,1,0:T(8,128)(2,1)}), bf16[64,96,128]{2,1,0:T(8,128)(2,1)}, u32[]{:S(2)}, u32[]{:S(2)}) async-start(bf16[64,96,128]{2,1,0:T(8,128)(2,1)} %bitcast.13), calls=%async_computation.1 | async-start | bytes 3145728 | tf_op jit(solution)/shard_map/all_to_all | solution.py:327
  70.6 1.4 %copy-done.5 = bf16[512,1536]{1,0:T(8,128)(2,1)S(1)} copy-done((bf16[512,1536]{1,0:T(8,128)(2,1)S(1)}, bf16[512,1536]{1,0:T(8,128)(2,1)}, u32[]{:S(2)}) %copy-start.5) | copy-done | bytes 1572888
  72.0 5.7 %shard_map.76.rest_0_ = f32[1,2,3072,512]{3,2,1,0:T(8,128)} custom-call(s32[4]{0:T(128)S(1)} %pad_add_fusion.1.place_ref, bf16[512,1536]{1,0:T(8,128)(2,1)S(1)} %shard_map.70.own_ref, bf16[512,1536]{1,0:T(8,128)(2,1)S(1)} %copy-done.5, bf16[512,512]{1,0:T(8,128)(2,1)S(1)} %get-tuple-element.39.dpre_ref.right_ref), custom_call_target="tpu_custom_call" | custom-call | flops 1610612736 | bytes 6291456 | tf_op jit(solution)/shard_map/pallas_call | solution.py:271
  77.7 5.7 %shard_map.77 = f32[1,2,3072,512]{3,2,1,0:T(8,128)} custom-call(s32[4]{0:T(128)S(1)} %pad_add_fusion.1.place_ref, bf16[512,1536]{1,0:T(8,128)(2,1)S(1)} %copy-done.3, bf16[512,1536]{1,0:T(8,128)(2,1)S(1)} %copy-done.7, bf16[512,512]{1,0:T(8,128)(2,1)S(1)} %get-tuple-element.38.right_ref, ...), custom_call_target="tpu_custom_call", output_to_operand_aliasing={{}: (4, {})} | custom-call | flops 1610612736 | bytes 6291456 | tf_op jit(solution)/shard_map/pallas_call | solution.py:271
  83.4 12.0 %all-to-all-done.1.parts_ref = bf16[64,96,128]{2,1,0:T(8,128)(2,1)} async-done(((bf16[64,96,128]{2,1,0:T(8,128)(2,1)}), bf16[64,96,128]{2,1,0:T(8,128)(2,1)}, u32[]{:S(2)}, u32[]{:S(2)}) %all-to-all-start.1) | async-done | bytes 1572896 | tf_op jit(solution)/shard_map/all_to_all | solution.py:327
  95.4 2.5 %shard_map.78 = bf16[192,128]{1,0:T(8,128)(2,1)} custom-call(bf16[64,96,128]{2,1,0:T(8,128)(2,1)} %all-to-all-done.1.parts_ref, bf16[512,128]{1,0:T(8,128)(2,1)S(1)} %get-tuple-element.41.hot_ref), custom_call_target="tpu_custom_call" | custom-call | tf_op jit(solution)/shard_map/pallas_call | solution.py:313
  (42 shorter events, 9.9 us)
Async XLA Ops:
  0.6 10.9 %copy-start = (bf16[128,3072]{1,0:T(8,128)(2,1)S(1)}, bf16[128,3072]{1,0:T(8,128)(2,1)}, u32[]{:S(2)}) copy-start(bf16[128,3072]{1,0:T(8,128)(2,1)} %param.5) | copy-start | bytes 2359300
  3.5 20.2 %all-to-all-start = ((bf16[8,64,384]{2,1,0:T(8,128)(2,1)}), bf16[8,64,384]{2,1,0:T(8,128)(2,1)S(1)}, u32[]{:S(2)}, u32[]{:S(2)}) async-start(bf16[8,64,384]{2,1,0:T(8,128)(2,1)} %bitcast.6), calls=%async_computation | async-start | bytes 786432 | tf_op jit(solution)/shard_map/all_to_all | solution.py:327
  12.9 10.8 %collective-permute-start = (bf16[64,1536]{1,0:T(8,128)(2,1)S(1)}, bf16[64,1536]{1,0:T(8,128)(2,1)S(1)}, u32[]{:S(2)}, u32[]{:S(2)}) collective-permute-start(bf16[64,1536]{1,0:T(8,128)(2,1)S(1)} %get-tuple-element.24), channel_id=1, source_target_pairs={{0,1},{1,2},{2,3},{3,0},{4,5},{5,6},{6,7},{7,4},{8,9},{9,10},{10,1... | collective-permute-start | bytes 589832 | tf_op jit(solution)/shard_map/ppermute | solution.py:337
  23.7 10.7 %collective-permute-start.9 = (bf16[512,384]{1,0:T(8,128)(2,1)S(1)}, bf16[512,384]{1,0:T(8,128)(2,1)S(1)}, u32[]{:S(2)}, u32[]{:S(2)}) collective-permute-start(bf16[512,384]{1,0:T(8,128)(2,1)S(1)} %bitcast.10), channel_id=1, source_target_pairs={{0,48},{16,0},{32,16},{48,32},{1,49},{17,1},{33,17},{49,33},{2,50}... | collective-permute-start | bytes 1179656 | tf_op jit(solution)/shard_map/ppermute | solution.py:343
  26.5 11.8 %collective-permute-start.8 = (bf16[512,384]{1,0:T(8,128)(2,1)S(1)}, bf16[512,384]{1,0:T(8,128)(2,1)S(1)}, u32[]{:S(2)}, u32[]{:S(2)}) collective-permute-start(bf16[512,384]{1,0:T(8,128)(2,1)S(1)} %bitcast.11), channel_id=1, source_target_pairs={{0,16},{16,32},{32,48},{48,0},{1,17},{17,33},{33,49},{49,1},{2,18}... | collective-permute-start | bytes 1179656 | tf_op jit(solution)/shard_map/ppermute | solution.py:343
  26.5 11.9 %collective-permute-start.1 = (bf16[64,1536]{1,0:T(8,128)(2,1)S(1)}, bf16[64,1536]{1,0:T(8,128)(2,1)S(1)}, u32[]{:S(2)}, u32[]{:S(2)}) collective-permute-start(bf16[64,1536]{1,0:T(8,128)(2,1)S(1)} %get-tuple-element.25), channel_id=1, source_target_pairs={{0,3},{1,0},{2,1},{3,2},{4,7},{5,4},{6,5},{7,6},{8,11},{9,8},{10,9... | collective-permute-start | bytes 589832 | tf_op jit(solution)/shard_map/ppermute | solution.py:337
  27.5 13.8 %collective-permute-start.2 = (bf16[64,1536]{1,0:T(8,128)(2,1)S(1)}, bf16[64,1536]{1,0:T(8,128)(2,1)S(1)}, u32[]{:S(2)}, u32[]{:S(2)}) collective-permute-start(bf16[64,1536]{1,0:T(8,128)(2,1)S(1)} %get-tuple-element.26), channel_id=1, source_target_pairs={{0,70},{1,71},{2,68},{3,69},{4,66},{5,67},{6,64},{7,65},{8,78},{9,... | collective-permute-start | bytes 589832 | tf_op jit(solution)/shard_map/ppermute | solution.py:337
  29.9 12.1 %collective-permute-start.3 = (bf16[64,1536]{1,0:T(8,128)(2,1)S(1)}, bf16[64,1536]{1,0:T(8,128)(2,1)S(1)}, u32[]{:S(2)}, u32[]{:S(2)}) collective-permute-start(bf16[64,1536]{1,0:T(8,128)(2,1)S(1)} %get-tuple-element.28), channel_id=1, source_target_pairs={{0,69},{1,70},{2,71},{3,68},{4,65},{5,66},{6,67},{7,64},{8,77},{9,... | collective-permute-start | bytes 589832 | tf_op jit(solution)/shard_map/ppermute | solution.py:337
  34.5 9.5 %collective-permute-start.10 = (bf16[256,384]{1,0:T(8,128)(2,1)S(1)}, bf16[256,384]{1,0:T(8,128)(2,1)S(1)}, u32[]{:S(2)}, u32[]{:S(2)}) collective-permute-start(bf16[256,384]{1,0:T(8,128)(2,1)S(1)} %slice.8), channel_id=1, source_target_pairs={{0,48},{16,0},{32,16},{48,32},{1,49},{17,1},{33,17},{49,33},{2,50}... | collective-permute-start | bytes 589832 | tf_op jit(solution)/shard_map/ppermute | solution.py:346
  38.2 6.9 %collective-permute-start.11 = (bf16[256,384]{1,0:T(8,128)(2,1)S(1)}, bf16[256,384]{1,0:T(8,128)(2,1)S(1)}, u32[]{:S(2)}, u32[]{:S(2)}) collective-permute-start(bf16[256,384]{1,0:T(8,128)(2,1)S(1)} %slice.9), channel_id=1, source_target_pairs={{0,16},{16,32},{32,48},{48,0},{1,17},{17,33},{33,49},{49,1},{2,18}... | collective-permute-start | bytes 589832 | tf_op jit(solution)/shard_map/ppermute | solution.py:347
  38.3 9.4 %collective-permute-start.4 = (bf16[64,1536]{1,0:T(8,128)(2,1)S(1)}, bf16[64,1536]{1,0:T(8,128)(2,1)S(1)}, u32[]{:S(2)}, u32[]{:S(2)}) collective-permute-start(bf16[64,1536]{1,0:T(8,128)(2,1)S(1)} %get-tuple-element.30), channel_id=1, source_target_pairs={{0,71},{1,68},{2,69},{3,70},{4,67},{5,64},{6,65},{7,66},{8,79},{9,... | collective-permute-start | bytes 589832 | tf_op jit(solution)/shard_map/ppermute | solution.py:337
  41.3 7.2 %collective-permute-start.5 = (bf16[64,1536]{1,0:T(8,128)(2,1)S(1)}, bf16[64,1536]{1,0:T(8,128)(2,1)S(1)}, u32[]{:S(2)}, u32[]{:S(2)}) collective-permute-start(bf16[64,1536]{1,0:T(8,128)(2,1)S(1)} %get-tuple-element.32), channel_id=1, source_target_pairs={{0,2},{1,3},{2,0},{3,1},{4,6},{5,7},{6,4},{7,5},{8,10},{9,11},{10,... | collective-permute-start | bytes 589832 | tf_op jit(solution)/shard_map/ppermute | solution.py:337
  42.0 7.9 %collective-permute-start.6 = (bf16[64,1536]{1,0:T(8,128)(2,1)S(1)}, bf16[64,1536]{1,0:T(8,128)(2,1)S(1)}, u32[]{:S(2)}, u32[]{:S(2)}) collective-permute-start(bf16[64,1536]{1,0:T(8,128)(2,1)S(1)} %get-tuple-element.34), channel_id=1, source_target_pairs={{0,68},{1,69},{2,70},{3,71},{4,64},{5,65},{6,66},{7,67},{8,76},{9,... | collective-permute-start | bytes 589832 | tf_op jit(solution)/shard_map/ppermute | solution.py:337
  45.2 5.4 %copy-start.1 = (bf16[1,2,3072,512]{3,2,1,0:T(8,128)(2,1)S(1)}, bf16[1,2,3072,512]{3,2,1,0:T(8,128)(2,1)}, u32[]{:S(2)}) copy-start(bf16[1,2,3072,512]{3,2,1,0:T(8,128)(2,1)} %panel_ref.7) | copy-start | bytes 18874372
  45.9 6.3 %copy-start.2 = (bf16[512,1536]{1,0:T(8,128)(2,1)}, bf16[512,1536]{1,0:T(8,128)(2,1)S(1)}, u32[]{:S(2)}) copy-start(bf16[512,1536]{1,0:T(8,128)(2,1)S(1)} %shard_map.72.own_ref) | copy-start | bytes 4718596
  45.9 6.3 %collective-permute-start.12 = (bf16[512,1536]{1,0:T(8,128)(2,1)S(1)}, bf16[512,1536]{1,0:T(8,128)(2,1)S(1)}, u32[]{:S(2)}, u32[]{:S(2)}) collective-permute-start(bf16[512,1536]{1,0:T(8,128)(2,1)S(1)} %shard_map.72.own_ref), channel_id=1, source_target_pairs={{0,8},{8,0},{1,9},{9,1},{2,10},{10,2},{3,11},{11,3},{4,12},{12,4},... | collective-permute-start | bytes 4718600 | tf_op jit(solution)/shard_map/ppermute | solution.py:350
  50.5 4.0 %collective-permute-start.7 = (bf16[512,1536]{1,0:T(8,128)(2,1)S(1)}, bf16[512,1536]{1,0:T(8,128)(2,1)S(1)}, u32[]{:S(2)}, u32[]{:S(2)}) collective-permute-start(bf16[512,1536]{1,0:T(8,128)(2,1)S(1)} %shard_map.70.own_ref), channel_id=1, source_target_pairs={{0,8},{8,0},{1,9},{9,1},{2,10},{10,2},{3,11},{11,3},{4,12},{12,4},... | collective-permute-start | bytes 4718600 | tf_op jit(solution)/shard_map/ppermute | solution.py:352
  52.2 2.3 %copy-start.6 = (bf16[512,1536]{1,0:T(8,128)(2,1)}, bf16[512,1536]{1,0:T(8,128)(2,1)S(1)}, u32[]{:S(2)}) copy-start(bf16[512,1536]{1,0:T(8,128)(2,1)S(1)} %collective-permute-done.12.oth_ref) | copy-start | bytes 4718596
  54.5 2.7 %copy-start.4 = (bf16[512,1536]{1,0:T(8,128)(2,1)}, bf16[512,1536]{1,0:T(8,128)(2,1)S(1)}, u32[]{:S(2)}) copy-start(bf16[512,1536]{1,0:T(8,128)(2,1)S(1)} %collective-permute-done.7.oth_ref) | copy-start | bytes 4718596
  57.3 3.6 %collective-permute-start.13 = (bf16[8,8,96,128]{3,2,1,0:T(8,128)(2,1)S(1)}, bf16[8,8,96,128]{3,2,1,0:T(8,128)(2,1)S(1)}, u32[]{:S(2)}, u32[]{:S(2)}) collective-permute-start(bf16[8,8,96,128]{3,2,1,0:T(8,128)(2,1)S(1)} %get-tuple-element.37), channel_id=1, source_target_pairs={{0,8},{8,0},{1,9},{9,1},{2,10},{10,2},{3,11},{11,3},{4,12},{12,4},... | collective-permute-start | bytes 4718600 | tf_op jit(solution)/shard_map/ppermute | solution.py:355
  62.5 32.9 %all-to-all-start.1 = ((bf16[64,96,128]{2,1,0:T(8,128)(2,1)}), bf16[64,96,128]{2,1,0:T(8,128)(2,1)}, u32[]{:S(2)}, u32[]{:S(2)}) async-start(bf16[64,96,128]{2,1,0:T(8,128)(2,1)} %bitcast.13), calls=%async_computation.1 | async-start | bytes 3145728 | tf_op jit(solution)/shard_map/all_to_all | solution.py:327
  70.5 1.4 %copy-start.5 = (bf16[512,1536]{1,0:T(8,128)(2,1)S(1)}, bf16[512,1536]{1,0:T(8,128)(2,1)}, u32[]{:S(2)}) copy-start(bf16[512,1536]{1,0:T(8,128)(2,1)} %copy-done.4) | copy-start | bytes 4718596
  72.0 5.7 %copy-start.3 = (bf16[512,1536]{1,0:T(8,128)(2,1)S(1)}, bf16[512,1536]{1,0:T(8,128)(2,1)}, u32[]{:S(2)}) copy-start(bf16[512,1536]{1,0:T(8,128)(2,1)} %copy-done.2) | copy-start | bytes 4718596
  72.0 5.7 %copy-start.7 = (bf16[512,1536]{1,0:T(8,128)(2,1)S(1)}, bf16[512,1536]{1,0:T(8,128)(2,1)}, u32[]{:S(2)}) copy-start(bf16[512,1536]{1,0:T(8,128)(2,1)} %copy-done.6) | copy-start | bytes 4718596
